TPU v7x, 128 devices: a whole 4x4x4 slice. The times are simulated.
128 devices in a mesh: dp: 8 (over y, core), ctx: 16 (over z, x).
Axes of the slice: x: 4, y: 4, z: 4, core: 2. Of those that a mesh axis runs over, the one named last changes fastest.
Arguments:
- query_act: bfloat16 [8, 2048, 8192], P('dp', 'ctx'), may hold values from -6 to 6
- key_act: bfloat16 [8, 2048, 8192], P('dp', 'ctx'), may hold values from -6 to 6
- value_act: bfloat16 [8, 2048, 8192], P('dp', 'ctx'), may hold values from -6 to 6
- grad_out: bfloat16 [8, 2048, 8192], P('dp', 'ctx'), may hold values from -6 to 6
- filter_taps: float32 [2048, 8192], P('ctx'), may hold values from -0.125 to 0.125
Outputs:
- grad_query: bfloat16 [8, 2048, 8192], P('dp', 'ctx')
- grad_key: bfloat16 [8, 2048, 8192], P('dp', 'ctx')
- grad_value: bfloat16 [8, 2048, 8192], P('dp', 'ctx')
- grad_filter: float32 [2048, 8192], P('dp', 'ctx')
All inputs are finite; a program needn't handle non-finite values.
Results may differ from a plain program's by a relative error of at most 0.017.
Values may be sent and summed in bfloat16 or wider, within the bound.
No kernel may reach another device: no remote copies, remote signals or barrier semaphores. Data moves between devices by JAX's collectives and lax.ppermute only.
A program may use at most 256 MiB of HBM per device.

v0:
```python
import math

import jax
import jax.numpy as jnp
from jax import lax
from jax.sharding import PartitionSpec as P

BLOCK = 64


def angle_table(rows_count, cols_count, modulus, sign):
    left = jnp.arange(rows_count, dtype=jnp.int32)
    right = jnp.arange(cols_count, dtype=jnp.int32)
    power = left[:, None] * right[None, :] % modulus
    angles = sign * 2.0 * math.pi * power.astype(jnp.float32) / modulus
    return (jnp.cos(angles), jnp.sin(angles))


def apply_first(table, operand):
    outer = operand.shape[0]
    flat = operand.reshape(outer, -1)
    result = jnp.dot(table, flat, precision=lax.Precision.HIGH, preferred_element_type=jnp.float32)
    return result.reshape(operand.shape)


def apply_second(table, operand):
    outer, inner, columns = operand.shape
    flat = operand.transpose(1, 0, 2).reshape(inner, outer * columns)
    result = jnp.dot(table, flat, precision=lax.Precision.HIGH, preferred_element_type=jnp.float32)
    return result.reshape(inner, outer, columns)


def transform(real_part, imag_part, sign, real_only):
    length_full = real_part.shape[0]
    columns = real_part.shape[1]
    outer = length_full // BLOCK
    real_block = real_part.reshape(outer, BLOCK, columns)
    cos_outer, sin_outer = angle_table(outer, outer, outer, sign)
    section_real = apply_first(cos_outer, real_block)
    section_imag = apply_first(sin_outer, real_block)
    if imag_part is not None:
        imag_block = imag_part.reshape(outer, BLOCK, columns)
        section_real = section_real - apply_first(sin_outer, imag_block)
        section_imag = section_imag + apply_first(cos_outer, imag_block)
    twist_cos, twist_sin = angle_table(outer, BLOCK, length_full, sign)
    turned_real = section_real * twist_cos[:, :, None] - section_imag * twist_sin[:, :, None]
    turned_imag = section_real * twist_sin[:, :, None] + section_imag * twist_cos[:, :, None]
    cos_inner, sin_inner = angle_table(BLOCK, BLOCK, BLOCK, sign)
    out_real = apply_second(cos_inner, turned_real) - apply_second(sin_inner, turned_imag)
    out_real = out_real.reshape(length_full, columns)
    if real_only:
        return (out_real, None)
    out_imag = apply_second(sin_inner, turned_real) + apply_second(cos_inner, turned_imag)
    return (out_real, out_imag.reshape(length_full, columns))


def on_device(query_act, key_act, value_act, grad_out, filter_taps):
    product = (key_act[0].astype(jnp.float32) * value_act[0].astype(jnp.float32)).astype(
        jnp.bfloat16
    )
    gated_grad = (grad_out[0].astype(jnp.float32) * query_act[0].astype(jnp.float32)).astype(
        jnp.bfloat16
    )
    prod_cols, grad_cols = (
        lax.all_to_all(product, "ctx", split_axis=1, concat_axis=0, tiled=True),
        lax.all_to_all(gated_grad, "ctx", split_axis=1, concat_axis=0, tiled=True),
    )
    taps_cols = lax.all_to_all(filter_taps, "ctx", split_axis=1, concat_axis=0, tiled=True)
    seq_len = prod_cols.shape[0]
    channels = prod_cols.shape[1]
    group_width = min(channels, 256)
    groups_count = channels // group_width
    length_full = 2 * seq_len
    padding = jnp.zeros((seq_len, 3 * group_width), jnp.float32)

    def group_step(group, buffers):
        conv_buf, back_buf, taps_buf = buffers
        start = group * group_width
        pieces = [
            lax.dynamic_slice_in_dim(source, start, group_width, 1).astype(jnp.float32)
            for source in (taps_cols, prod_cols, grad_cols)
        ]
        stacked = jnp.concatenate([jnp.concatenate(pieces, axis=1), padding], axis=0)
        spec_real, spec_imag = transform(stacked, None, -1.0, False)
        taps_re = spec_real[:, :group_width]
        taps_im = spec_imag[:, :group_width]
        prod_re = spec_real[:, group_width : 2 * group_width]
        prod_im = spec_imag[:, group_width : 2 * group_width]
        grad_re = spec_real[:, 2 * group_width :]
        grad_im = spec_imag[:, 2 * group_width :]
        mixed_real = jnp.concatenate(
            [
                taps_re * prod_re - taps_im * prod_im,
                taps_re * grad_re + taps_im * grad_im,
                prod_re * grad_re + prod_im * grad_im,
            ],
            axis=1,
        )
        mixed_imag = jnp.concatenate(
            [
                taps_re * prod_im + taps_im * prod_re,
                taps_re * grad_im - taps_im * grad_re,
                prod_re * grad_im - prod_im * grad_re,
            ],
            axis=1,
        )
        back_real, unused = transform(mixed_real, mixed_imag, 1.0, True)
        back_real = back_real[:seq_len] / length_full
        conv_buf = lax.dynamic_update_slice_in_dim(
            conv_buf, back_real[:, :group_width].astype(jnp.bfloat16), start, 1
        )
        back_buf = lax.dynamic_update_slice_in_dim(
            back_buf, back_real[:, group_width : 2 * group_width].astype(jnp.bfloat16), start, 1
        )
        taps_buf = lax.dynamic_update_slice_in_dim(
            taps_buf, back_real[:, 2 * group_width :], start, 1
        )
        return (conv_buf, back_buf, taps_buf)

    initial = (
        jnp.zeros((seq_len, channels), jnp.bfloat16),
        jnp.zeros((seq_len, channels), jnp.bfloat16),
        jnp.zeros((seq_len, channels), jnp.float32),
    )
    conv_cols, back_cols, taps_grad = lax.fori_loop(0, groups_count, group_step, initial)
    conv_seq, back_seq = (
        lax.all_to_all(conv_cols, "ctx", split_axis=0, concat_axis=1, tiled=True),
        lax.all_to_all(back_cols, "ctx", split_axis=0, concat_axis=1, tiled=True),
    )
    grad_filter = lax.psum_scatter(
        taps_grad.astype(jnp.bfloat16), "dp", scatter_dimension=0, tiled=True
    ).astype(jnp.float32)
    grad_query = (grad_out[0].astype(jnp.float32) * conv_seq.astype(jnp.float32)).astype(
        jnp.bfloat16
    )
    grad_key = (back_seq.astype(jnp.float32) * value_act[0].astype(jnp.float32)).astype(
        jnp.bfloat16
    )
    grad_value = (back_seq.astype(jnp.float32) * key_act[0].astype(jnp.float32)).astype(
        jnp.bfloat16
    )
    return (grad_query[None], grad_key[None], grad_value[None], grad_filter)


def solution(mesh):
    in_specs = (
        P("dp", "ctx", None),
        P("dp", "ctx", None),
        P("dp", "ctx", None),
        P("dp", "ctx", None),
        P("ctx", None),
    )
    out_specs = (P("dp", "ctx", None), P("dp", "ctx", None), P("dp", "ctx", None), P("dp", "ctx"))
    return jax.shard_map(
        on_device, mesh=mesh, in_specs=in_specs, out_specs=out_specs, check_vma=False
    )
```

profile of v0, /device:TPU:1, one launch (start us, length us, event | category | flops | bytes accessed | tf_op | source)
XLA Modules:
  0.0 914.0 jit_solution(16216452031411015211)
XLA Ops:
  70.4 21.9 %all-to-all-done.2 = bf16[128,16,512]{2,0,1:T(8,128)(2,1)} async-done(((bf16[128,16,512]{2,0,1:T(8,128)(2,1)}), bf16[128,16,512]{2,0,1:T(8,128)(2,1)}, u32[]{:S(2)}, u32[]{:S(2)}) %all-to-all-start.2) | async-done | bytes 2097184 | tf_op jit(solution)/shard_map/all_to_all | solution.py:66
  99.3 58.7 %all-to-all-done = f32[128,16,512]{2,0,1:T(8,128)} async-done(((f32[128,16,512]{2,0,1:T(8,128)}), f32[128,16,512]{2,0,1:T(8,128)}, u32[]{:S(2)}, u32[]{:S(2)}) %all-to-all-start) | async-done | bytes 4194336 | tf_op jit(solution)/shard_map/all_to_all | solution.py:68
  162.4 668.5 %while.20 = (s32[]{:T(128)}, bf16[2048,512]{1,0:T(8,128)(2,1)}, bf16[2048,512]{1,0:T(8,128)(2,1)}, bf16[2048,512]{1,0:T(8,128)(2,1)}, f32[2048,512]{1,0:T(8,128)...) while((s32[]{:T(128)}, bf16[2048,512]{1,0:T(8,128)(2,1)}, ...), condition=%wide.region_1.2_spmd, body=%wide.region_0.1_spmd.sunk | while | flops 14602862592 | bytes 997327168 | solution.py:125
  199.4 17.9 %fusion.199 = (f32[64,64,768]{2,1,0:T(8,128)}, f32[64,64,768]{2,1,0:T(8,128)}) fusion(f32[64,64,768]{2,0,1:T(8,128)} %fusion.198, f32[64,64]{1,0:T(8,128)S(1)} %multiply_sine_fusion.13, f32[64,64]{1,0:T(8,128)S(1)} %multiply_cosine_fusion.13, f32[8,64,8,768]{3,2,1,0:T(8,128)} %bitcast.267), kind=kOutput, calls=%fused_computation.39.clone.1 | convolution fusion | flops 1226891264 | bytes 50364416 | tf_op jit(solution)/shard_map/while/body/eval_jaxpr/dot_general | solution.py:22
  217.3 20.8 %fusion.202 = f32[64,64,768]{2,0,1:T(8,128)} fusion(f32[8,8,64,768]{3,2,1,0:T(8,128)} %bitcast.272), kind=kOutput, calls=%fused_computation.16.clone.1 | convolution fusion | flops 1208016896 | bytes 25165824 | tf_op jit(solution)/shard_map/while/body/eval_jaxpr/dot_general | solution.py:29
  238.0 17.2 %fusion.203 = f32[64,64,768]{2,0,1:T(8,128)} fusion(f32[64,64,768]{2,0,1:T(8,128)} %fusion.202, f32[8,8,64,768]{3,2,1,0:T(8,128)S(1)} %bitcast.277), kind=kOutput, calls=%fused_computation.55.clone.1 | convolution fusion | flops 1211162624 | bytes 37748736 | tf_op jit(solution)/shard_map/while/body/eval_jaxpr/dot_general | solution.py:29
  255.3 16.4 %copy.203 = f32[64,64,768]{2,1,0:T(8,128)} copy(f32[64,64,768]{2,0,1:T(8,128)} %fusion.203) | data formatting | bytes 25165824 | tf_op jit(solution)/shard_map/while/body/eval_jaxpr/sub | solution.py:49
  271.7 18.9 %fusion.200 = f32[64,64,768]{2,0,1:T(8,128)S(1)} fusion(f32[8,8,64,768]{3,2,1,0:T(8,128)} %bitcast.273), kind=kOutput, calls=%fused_computation.14.clone.1 | convolution fusion | flops 1208016896 | bytes 25165824 | tf_op jit(solution)/shard_map/while/body/eval_jaxpr/dot_general | solution.py:29
  290.5 21.5 %fusion.201 = f32[64,64,768]{2,0,1:T(8,128)} fusion(f32[64,64,768]{2,0,1:T(8,128)S(1)} %fusion.200, f32[8,8,64,768]{3,2,1,0:T(8,128)} %bitcast.276), kind=kOutput, calls=%fused_computation.56.clone.1 | convolution fusion | flops 1211162624 | bytes 37748736 | tf_op jit(solution)/shard_map/while/body/eval_jaxpr/dot_general | solution.py:29
  312.0 16.4 %copy.202 = f32[64,64,768]{2,1,0:T(8,128)} copy(f32[64,64,768]{2,0,1:T(8,128)} %fusion.201) | data formatting | bytes 25165824 | tf_op jit(solution)/shard_map/while/body/eval_jaxpr/add | solution.py:53
  424.8 27.5 %fusion.207 = (f32[64,64,768]{2,1,0:T(8,128)}, f32[64,64,768]{2,1,0:T(8,128)}) fusion(f32[64,64]{1,0:T(8,128)S(1)} %multiply_sine_fusion.12, f32[64,64]{1,0:T(8,128)S(1)} %multiply_cosine_fusion.12, f32[64,64,768]{2,0,1:T(8,128)} %fusion.204, f32[64,64,768]{2,0,1:T(8,128)} %fusion.205, f32[64,64,768]{2,0,1:T(8,128)} %fusion.206, ...), kind=kOutput, calls=%fused_computation.33.clone.1 | convolution fusion | flops 1233182720 | bytes 75530240 | tf_op jit(solution)/shard_map/while/body/eval_jaxpr/dot_general | solution.py:22
  452.3 18.5 %fusion.208 = f32[64,64,768]{2,0,1:T(8,128)S(1)} fusion(f32[8,8,64,768]{3,2,1,0:T(8,128)} %bitcast.279), kind=kOutput, calls=%fused_computation.clone.1 | convolution fusion | flops 1208016896 | bytes 25165824 | tf_op jit(solution)/shard_map/while/body/eval_jaxpr/dot_general | solution.py:29
  470.9 14.9 %fusion.209 = f32[64,64,768]{2,0,1:T(8,128)} fusion(f32[8,8,64,768]{3,2,1,0:T(8,128)S(1)} %bitcast.278), kind=kOutput, calls=%fused_computation.3.clone.1 | convolution fusion | flops 1208016896 | bytes 25165824 | tf_op jit(solution)/shard_map/while/body/eval_jaxpr/dot_general | solution.py:29
  532.1 17.9 %fusion.199 = (f32[64,64,768]{2,1,0:T(8,128)}, f32[64,64,768]{2,1,0:T(8,128)}) fusion(f32[64,64,768]{2,0,1:T(8,128)} %fusion.198, f32[64,64]{1,0:T(8,128)S(1)} %multiply_sine_fusion.13, f32[64,64]{1,0:T(8,128)S(1)} %multiply_cosine_fusion.13, f32[8,64,8,768]{3,2,1,0:T(8,128)} %bitcast.267), kind=kOutput, calls=%fused_computation.39.clone.1 | convolution fusion | flops 1226891264 | bytes 50364416 | tf_op jit(solution)/shard_map/while/body/eval_jaxpr/dot_general | solution.py:22
  550.0 20.4 %fusion.202 = f32[64,64,768]{2,0,1:T(8,128)} fusion(f32[8,8,64,768]{3,2,1,0:T(8,128)} %bitcast.272), kind=kOutput, calls=%fused_computation.16.clone.1 | convolution fusion | flops 1208016896 | bytes 25165824 | tf_op jit(solution)/shard_map/while/body/eval_jaxpr/dot_general | solution.py:29
  570.4 17.5 %fusion.203 = f32[64,64,768]{2,0,1:T(8,128)} fusion(f32[64,64,768]{2,0,1:T(8,128)} %fusion.202, f32[8,8,64,768]{3,2,1,0:T(8,128)S(1)} %bitcast.277), kind=kOutput, calls=%fused_computation.55.clone.1 | convolution fusion | flops 1211162624 | bytes 37748736 | tf_op jit(solution)/shard_map/while/body/eval_jaxpr/dot_general | solution.py:29
  587.8 16.4 %copy.203 = f32[64,64,768]{2,1,0:T(8,128)} copy(f32[64,64,768]{2,0,1:T(8,128)} %fusion.203) | data formatting | bytes 25165824 | tf_op jit(solution)/shard_map/while/body/eval_jaxpr/sub | solution.py:49
  604.2 18.8 %fusion.200 = f32[64,64,768]{2,0,1:T(8,128)S(1)} fusion(f32[8,8,64,768]{3,2,1,0:T(8,128)} %bitcast.273), kind=kOutput, calls=%fused_computation.14.clone.1 | convolution fusion | flops 1208016896 | bytes 25165824 | tf_op jit(solution)/shard_map/while/body/eval_jaxpr/dot_general | solution.py:29
  623.0 21.4 %fusion.201 = f32[64,64,768]{2,0,1:T(8,128)} fusion(f32[64,64,768]{2,0,1:T(8,128)S(1)} %fusion.200, f32[8,8,64,768]{3,2,1,0:T(8,128)} %bitcast.276), kind=kOutput, calls=%fused_computation.56.clone.1 | convolution fusion | flops 1211162624 | bytes 37748736 | tf_op jit(solution)/shard_map/while/body/eval_jaxpr/dot_general | solution.py:29
  644.4 16.4 %copy.202 = f32[64,64,768]{2,1,0:T(8,128)} copy(f32[64,64,768]{2,0,1:T(8,128)} %fusion.201) | data formatting | bytes 25165824 | tf_op jit(solution)/shard_map/while/body/eval_jaxpr/add | solution.py:53
  757.3 27.5 %fusion.207 = (f32[64,64,768]{2,1,0:T(8,128)}, f32[64,64,768]{2,1,0:T(8,128)}) fusion(f32[64,64]{1,0:T(8,128)S(1)} %multiply_sine_fusion.12, f32[64,64]{1,0:T(8,128)S(1)} %multiply_cosine_fusion.12, f32[64,64,768]{2,0,1:T(8,128)} %fusion.204, f32[64,64,768]{2,0,1:T(8,128)} %fusion.205, f32[64,64,768]{2,0,1:T(8,128)} %fusion.206, ...), kind=kOutput, calls=%fused_computation.33.clone.1 | convolution fusion | flops 1233182720 | bytes 75530240 | tf_op jit(solution)/shard_map/while/body/eval_jaxpr/dot_general | solution.py:22
  784.7 18.5 %fusion.208 = f32[64,64,768]{2,0,1:T(8,128)S(1)} fusion(f32[8,8,64,768]{3,2,1,0:T(8,128)} %bitcast.279), kind=kOutput, calls=%fused_computation.clone.1 | convolution fusion | flops 1208016896 | bytes 25165824 | tf_op jit(solution)/shard_map/while/body/eval_jaxpr/dot_general | solution.py:29
  803.3 14.9 %fusion.209 = f32[64,64,768]{2,0,1:T(8,128)} fusion(f32[8,8,64,768]{3,2,1,0:T(8,128)S(1)} %bitcast.278), kind=kOutput, calls=%fused_computation.3.clone.1 | convolution fusion | flops 1208016896 | bytes 25165824 | tf_op jit(solution)/shard_map/while/body/eval_jaxpr/dot_general | solution.py:29
  836.2 24.3 %all-to-all-done.4 = bf16[16,128,512]{2,1,0:T(8,128)(2,1)} async-done(((bf16[16,128,512]{2,1,0:T(8,128)(2,1)}), bf16[16,128,512]{2,1,0:T(8,128)(2,1)}, u32[]{:S(2)}, u32[]{:S(2)}) %all-to-all-start.4) | async-done | bytes 2097184 | tf_op jit(solution)/shard_map/all_to_all | solution.py:128
  (126 shorter events, 411.1 us)
Async XLA Ops:
  10.4 11.9 %copy-start.10 = (bf16[1,128,8192]{1,2,0:T(8,128)(2,1)}, bf16[1,128,8192]{1,2,0:T(8,128)(2,1)S(1)}, u32[]{:S(2)}) copy-start(bf16[1,128,8192]{1,2,0:T(8,128)(2,1)S(1)} %copy.67) | copy-start | bytes 6291460
  22.3 38.9 %all-to-all-start.1 = ((bf16[128,16,512]{2,0,1:T(8,128)(2,1)}), bf16[128,16,512]{2,0,1:T(8,128)(2,1)S(1)}, u32[]{:S(2)}, u32[]{:S(2)}) async-start(bf16[128,16,512]{2,0,1:T(8,128)(2,1)} %copy.69), calls=%async_computation.1 | async-start | bytes 4194304 | tf_op jit(solution)/shard_map/all_to_all | solution.py:65
  61.2 31.2 %all-to-all-start.2 = ((bf16[128,16,512]{2,0,1:T(8,128)(2,1)}), bf16[128,16,512]{2,0,1:T(8,128)(2,1)}, u32[]{:S(2)}, u32[]{:S(2)}) async-start(bf16[128,16,512]{2,0,1:T(8,128)(2,1)} %copy.71), calls=%async_computation.2 | async-start | bytes 4194304 | tf_op jit(solution)/shard_map/all_to_all | solution.py:66
  92.4 65.6 %all-to-all-start = ((f32[128,16,512]{2,0,1:T(8,128)}), f32[128,16,512]{2,0,1:T(8,128)}, u32[]{:S(2)}, u32[]{:S(2)}) async-start(f32[128,16,512]{2,0,1:T(8,128)} %bitcast.284), calls=%async_computation | async-start | bytes 8388608 | tf_op jit(solution)/shard_map/all_to_all | solution.py:68
  217.3 20.8 %copy-start.2 = (f32[64,64,768]{2,1,0:T(8,128)S(1)}, f32[64,64,768]{2,1,0:T(8,128)}, u32[]{:S(2)}) copy-start(f32[64,64,768]{2,1,0:T(8,128)} %get-tuple-element.313) | copy-start | bytes 37748740 | tf_op jit(solution)/shard_map/while
  328.4 15.0 %copy-start.1 = (f32[64,64,768]{2,1,0:T(8,128)S(1)}, f32[64,64,768]{2,1,0:T(8,128)}, u32[]{:S(2)}) copy-start(f32[64,64,768]{2,1,0:T(8,128)} %copy.202) | copy-start | bytes 37748740 | tf_op jit(solution)/shard_map/while
  375.3 11.7 %copy-start.4 = (f32[4096,256]{1,0:T(8,128)S(1)}, f32[4096,256]{1,0:T(8,128)}, u32[]{:S(2)}) copy-start(f32[4096,256]{1,0:T(8,128)} %get-tuple-element.316) | copy-start | bytes 12582916 | tf_op jit(solution)/shard_map/while
  375.3 11.7 %copy-start.5 = (f32[4096,256]{1,0:T(8,128)S(1)}, f32[4096,256]{1,0:T(8,128)}, u32[]{:S(2)}) copy-start(f32[4096,256]{1,0:T(8,128)} %get-tuple-element.315) | copy-start | bytes 12582916 | tf_op jit(solution)/shard_map/while
  375.3 11.7 %copy-start.6 = (f32[4096,256]{1,0:T(8,128)S(1)}, f32[4096,256]{1,0:T(8,128)}, u32[]{:S(2)}) copy-start(f32[4096,256]{1,0:T(8,128)} %get-tuple-element.314) | copy-start | bytes 12582916 | tf_op jit(solution)/shard_map/while
  403.8 11.6 %copy-start = (f32[64,49152]{1,0:T(8,128)S(1)}, f32[64,49152]{1,0:T(8,128)}, u32[]{:S(2)}) copy-start(f32[64,49152]{1,0:T(8,128)} %reshape.343) | copy-start | bytes 37748740 | tf_op jit(solution)/shard_map/while
  452.3 18.6 %copy-start.3 = (f32[64,64,768]{2,1,0:T(8,128)S(1)}, f32[64,64,768]{2,1,0:T(8,128)}, u32[]{:S(2)}) copy-start(f32[64,64,768]{2,1,0:T(8,128)} %get-tuple-element.321) | copy-start | bytes 37748740 | tf_op jit(solution)/shard_map/while
  485.8 6.1 copy-start.12
  550.0 20.4 %copy-start.2 = (f32[64,64,768]{2,1,0:T(8,128)S(1)}, f32[64,64,768]{2,1,0:T(8,128)}, u32[]{:S(2)}) copy-start(f32[64,64,768]{2,1,0:T(8,128)} %get-tuple-element.313) | copy-start | bytes 37748740 | tf_op jit(solution)/shard_map/while
  660.8 15.0 %copy-start.1 = (f32[64,64,768]{2,1,0:T(8,128)S(1)}, f32[64,64,768]{2,1,0:T(8,128)}, u32[]{:S(2)}) copy-start(f32[64,64,768]{2,1,0:T(8,128)} %copy.202) | copy-start | bytes 37748740 | tf_op jit(solution)/shard_map/while
  707.7 11.7 %copy-start.4 = (f32[4096,256]{1,0:T(8,128)S(1)}, f32[4096,256]{1,0:T(8,128)}, u32[]{:S(2)}) copy-start(f32[4096,256]{1,0:T(8,128)} %get-tuple-element.316) | copy-start | bytes 12582916 | tf_op jit(solution)/shard_map/while
  707.7 11.7 %copy-start.5 = (f32[4096,256]{1,0:T(8,128)S(1)}, f32[4096,256]{1,0:T(8,128)}, u32[]{:S(2)}) copy-start(f32[4096,256]{1,0:T(8,128)} %get-tuple-element.315) | copy-start | bytes 12582916 | tf_op jit(solution)/shard_map/while
  707.7 11.7 %copy-start.6 = (f32[4096,256]{1,0:T(8,128)S(1)}, f32[4096,256]{1,0:T(8,128)}, u32[]{:S(2)}) copy-start(f32[4096,256]{1,0:T(8,128)} %get-tuple-element.314) | copy-start | bytes 12582916 | tf_op jit(solution)/shard_map/while
  736.3 11.6 %copy-start = (f32[64,49152]{1,0:T(8,128)S(1)}, f32[64,49152]{1,0:T(8,128)}, u32[]{:S(2)}) copy-start(f32[64,49152]{1,0:T(8,128)} %reshape.343) | copy-start | bytes 37748740 | tf_op jit(solution)/shard_map/while
  784.7 18.6 %copy-start.3 = (f32[64,64,768]{2,1,0:T(8,128)S(1)}, f32[64,64,768]{2,1,0:T(8,128)}, u32[]{:S(2)}) copy-start(f32[64,64,768]{2,1,0:T(8,128)} %get-tuple-element.321) | copy-start | bytes 37748740 | tf_op jit(solution)/shard_map/while
  830.9 42.8 %copy-start.11 = (bf16[1,128,8192]{1,2,0:T(8,128)(2,1)S(1)}, bf16[1,128,8192]{1,2,0:T(8,128)(2,1)}, u32[]{:S(2)}) copy-start(bf16[1,128,8192]{1,2,0:T(8,128)(2,1)} %copy-done.10) | copy-start | bytes 6291460
  830.9 29.6 %all-to-all-start.4 = ((bf16[16,128,512]{2,1,0:T(8,128)(2,1)}), bf16[16,128,512]{2,1,0:T(8,128)(2,1)}, u32[]{:S(2)}, u32[]{:S(2)}) async-start(bf16[16,128,512]{2,1,0:T(8,128)(2,1)} %bitcast.289), calls=%async_computation.4 | async-start | bytes 4194304 | tf_op jit(solution)/shard_map/all_to_all | solution.py:128
  835.5 69.6 %reduce-scatter.2.cloned.1.call-start = ((), (), s32[]{:S(2)}) async-start(), calls=%async_computation.6 | async-start | bytes 2359296 | tf_op jit(solution)/shard_map/reduce_scatter | solution.py:130
  860.5 32.7 %all-to-all-start.3 = ((bf16[16,128,512]{2,1,0:T(8,128)(2,1)}), bf16[16,128,512]{2,1,0:T(8,128)(2,1)}, u32[]{:S(2)}, u32[]{:S(2)}) async-start(bf16[16,128,512]{2,1,0:T(8,128)(2,1)} %bitcast.288), calls=%async_computation.3 | async-start | bytes 4194304 | tf_op jit(solution)/shard_map/all_to_all | solution.py:127
  878.1 21.0 %copy-start.9 = (bf16[1,128,8192]{1,2,0:T(8,128)(2,1)S(1)}, bf16[1,128,8192]{1,2,0:T(8,128)(2,1)}, u32[]{:S(2)}) copy-start(bf16[1,128,8192]{1,2,0:T(8,128)(2,1)} %copy.65) | copy-start | bytes 6291460
  (7 other events, 23.2 us)
Sparse Core Ops, SparseCore 0:
  838.7 35.3 reduce-scatter.1
where the time goes:
time: 925 us; the launch traced here: 914 us
  matrix products  402 us (43%)
  local copies, waits for them, and re-layouts  209 us (23%)
  waiting for transfers between devices  127 us (14%)
  other arithmetic  126 us (14%)
  starting transfers between devices  31.7 us (3%)
  between operations  14.4 us (2%)
    dot_general x12, matrix products, apply_second(): jnp.dot(table, flat, precision=lax.Precision.HIGH, preferred_element_type...  223 us
    dot_general x12, matrix products, apply_first(): jnp.dot(table, flat, precision=lax.Precision.HIGH, preferred_element_type...  179 us
    reshape x6, local copies, waits for them, and re-layouts, apply_first(): flat = operand.reshape(outer, -1)  71.9 us
    all_to_all x1, waiting for transfers between devices, on_device(): lax.all_to_all(filter_taps, 'ctx', split_axis=1, concat_axis=0, tiled=True)  58.7 us
    add x2, local copies, waits for them, and re-layouts, transform(): apply_second(sin_inner, turned_real) + apply_second(cos_inner, turned_imag)  32.8 us
    sub x2, local copies, waits for them, and re-layouts, transform(): apply_second(cos_inner, turned_real) - apply_second(sin_inner, turned_imag)  32.7 us
    unnamed x13, local copies, waits for them, and re-layouts  28.2 us
    sub x2, other arithmetic, group_step(): taps_re * prod_re - taps_im * prod_im  26.2 us
  transfers between devices with their start and end apart: 6, of which 5 were waited for; matrix products, arithmetic and copies ran while one was open for 6% of the time, Pallas kernels for 0%

commit v1 on v0

v1 whole, which is shorter than its diff:
```python
import functools

import jax
import jax.numpy as jnp
from jax import lax
from jax.experimental import pallas as pl
from jax.experimental.pallas import tpu as pltpu
from jax.sharding import PartitionSpec as P

LANES = 128
NT = (((1,), (1,)), ((), ()))


def params(mib):
    return pltpu.CompilerParams(vmem_limit_bytes=mib * 1024 * 1024)


def grid_of(shape):
    return lax.broadcasted_iota(jnp.int32, shape, 0), lax.broadcasted_iota(jnp.int32, shape, 1)


def ones_where(condition):
    return jnp.where(condition, 1.0, 0.0).astype(jnp.bfloat16)


def identity():
    rows, cols = grid_of((LANES, LANES))
    return ones_where(rows == cols)


def reversal():
    rows, cols = grid_of((LANES, LANES))
    return ones_where(rows + cols == LANES - 1)


def turn(matrix, array):
    return lax.dot_general(matrix, array, NT, preferred_element_type=jnp.float32)


def gate(left, right):
    return (left.astype(jnp.float32) * right.astype(jnp.float32)).astype(jnp.bfloat16)


def send_body(local, share, key_ref, value_ref, grad_ref, query_ref, taps_ref, out_ref):
    per = LANES // local
    same = identity()
    rows, cols = grid_of((per * share, LANES))
    first = lax.axis_index("dp") * share
    pick = ones_where(cols == rows // share * local + first + rows % share)
    for g in range(key_ref.shape[1] // LANES):
        at = slice(g * LANES, (g + 1) * LANES)
        product = turn(same, gate(key_ref[:, at], value_ref[:, at])).astype(jnp.bfloat16)
        gated = turn(same, gate(grad_ref[:, at], query_ref[:, at])).astype(jnp.bfloat16)
        taps = turn(pick, taps_ref[:, at].astype(jnp.bfloat16)).astype(jnp.bfloat16)
        for d in range(per):
            dest = g * per + d
            out_ref[dest, :local, :] = product[d * local : (d + 1) * local]
            out_ref[dest, local : 2 * local, :] = gated[d * local : (d + 1) * local]
            out_ref[dest, 2 * local :, :] = taps[d * share : (d + 1) * share]


def send(key, value, grad, query, taps, local, share):
    length, channels = key.shape
    width = 2048
    message = 2 * local + share
    spec = pl.BlockSpec((length, width), lambda g: (0, g))
    return pl.pallas_call(
        functools.partial(send_body, local, share),
        grid=(channels // width,),
        in_specs=[spec] * 5,
        out_specs=pl.BlockSpec((width // local, message, LANES), lambda g: (g, 0, 0)),
        out_shape=jax.ShapeDtypeStruct((channels // local, message, LANES), jnp.bfloat16),
        compiler_params=params(60),
        cost_estimate=pl.CostEstimate(flops=0, bytes_accessed=20_000_000, transcendentals=0),
        name="send",
    )(key, value, grad, query, taps)


def both_body(
    local, share, seqs, group, prod_ref, grad_ref, taps_ref, out_ref, prod_wide, grad_wide, taps_wide, taps
):
    rows = prod_ref.shape[0]
    blocks = rows // seqs
    flip = reversal()
    g = pl.program_id(0)

    @pl.when(g == 0)
    def _():
        taps_wide[...] = taps_ref[...].astype(jnp.float32).reshape(rows * share, LANES)
        for c in range(local):
            taps[c * blocks : (c + 1) * blocks, :] = taps_wide[pl.ds(c, blocks, stride=seqs * share), :]

    prod_wide[...] = prod_ref[...].astype(jnp.float32).reshape(rows * group, LANES)
    grad_wide[...] = jnp.dot(
        grad_ref[...].reshape(rows * group, LANES), flip, preferred_element_type=jnp.float32
    )
    row, lane = grid_of((LANES, LANES))
    same_block = lane >= row

    def step(c, carry):
        here = pl.ds(c, rows, stride=group)
        prod = prod_wide[here, :].astype(jnp.bfloat16)
        grad = grad_wide[here, :].astype(jnp.bfloat16)
        before = jnp.zeros((LANES, LANES), jnp.float32)
        conv = [None] * blocks
        back = [None] * blocks

        def add(sums, i, piece):
            sums[i] = piece if sums[i] is None else sums[i] + piece

        for k in range(0, blocks, 2):
            pair = []
            for near in (k, k + 1):
                line = taps[pl.ds((g * group + c) * blocks + near, 1), :]
                turned = pltpu.roll(
                    jnp.broadcast_to(line, (LANES, LANES)), 0, 1, stride=1, stride_axis=0
                )
                pair.append(jnp.where(same_block, turned, before).astype(jnp.bfloat16))
                before = turned
            used = rows - k * seqs
            lines = jnp.concatenate([prod[:used], grad[k * seqs :]], axis=0)
            part = jnp.dot(
                lines, jnp.concatenate(pair, axis=1), preferred_element_type=jnp.float32
            )
            for j in range(blocks - k):
                for side in (0, 1):
                    cols = slice(side * LANES, (side + 1) * LANES)
                    if j + k + side < blocks:
                        add(conv, j + k + side, part[j * seqs : (j + 1) * seqs, cols])
                    if j >= side:
                        add(back, j - side, part[used + j * seqs : used + (j + 1) * seqs, cols])
        prod_wide[here, :] = jnp.concatenate(conv, axis=0)
        grad_wide[here, :] = jnp.concatenate(back, axis=0)
        return carry

    lax.fori_loop(0, group, step, 0, unroll=True)
    out_ref[:, 0] = prod_wide[...].astype(jnp.bfloat16).reshape(rows, group, LANES)
    rounded = grad_wide[...].astype(jnp.bfloat16)
    out_ref[:, 1] = (
        jnp.dot(rounded, flip, preferred_element_type=jnp.float32)
        .astype(jnp.bfloat16)
        .reshape(rows, group, LANES)
    )


def both(received, local, share, seqs):
    rows = received.shape[0]
    blocks = rows // seqs
    group = 8
    steps = local // group
    return pl.pallas_call(
        functools.partial(both_body, local, share, seqs, group),
        grid=(steps,),
        in_specs=[
            pl.BlockSpec((rows, group, LANES), lambda g: (0, g, 0)),
            pl.BlockSpec((rows, group, LANES), lambda g: (0, steps + g, 0)),
            pl.BlockSpec((rows, share, LANES), lambda g: (0, 2 * local // share, 0)),
        ],
        out_specs=pl.BlockSpec((rows, 2, group, LANES), lambda g: (0, 0, g, 0)),
        out_shape=jax.ShapeDtypeStruct((rows, 2, local, LANES), jnp.bfloat16),
        scratch_shapes=[
            pltpu.VMEM((rows * group, LANES), jnp.float32),
            pltpu.VMEM((rows * group, LANES), jnp.float32),
            pltpu.VMEM((rows * share, LANES), jnp.float32),
            pltpu.VMEM((local * blocks, LANES), jnp.float32),
        ],
        compiler_params=params(40),
        cost_estimate=pl.CostEstimate(
            flops=20_000_000_000, bytes_accessed=10_000_000, transcendentals=0
        ),
        name="both",
    )(received, received, received)


def filter_body(local, seqs, group, prod_ref, grad_ref, out_ref, prod_wide, grad_wide, padded):
    rows = prod_ref.shape[0]
    blocks = rows // seqs
    flip = reversal()
    row, lane = grid_of((LANES, LANES))
    same_block = lane <= row
    prod_wide[...] = prod_ref[...].astype(jnp.float32).reshape(rows * group, LANES)
    grad_wide[...] = grad_ref[...].astype(jnp.float32).reshape(rows * group, LANES)
    padded[:, rows:, :] = jnp.zeros((2, rows, LANES), jnp.float32)

    def step(c, carry):
        here = pl.ds(c, rows, stride=group)
        lines = turn(flip, prod_wide[here, :].astype(jnp.bfloat16)).astype(jnp.bfloat16)
        slot = padded.at[c % 2]
        slot[:rows, :] = grad_wide[here, :]
        after = jnp.zeros((LANES, LANES), jnp.float32)
        for k in reversed(range(0, blocks, 2)):
            pair = jnp.concatenate(
                [
                    slot[near * seqs : near * seqs + rows, :].astype(jnp.bfloat16)
                    for near in (k, k + 1)
                ],
                axis=1,
            )
            part = jnp.dot(lines, pair, preferred_element_type=jnp.float32)
            for side in (1, 0):
                turned = pltpu.roll(
                    part[:, side * LANES : (side + 1) * LANES], 1, 1, stride=1, stride_axis=0
                )
                chosen = jnp.where(same_block, turned, after)
                out_ref[k + side, pl.ds(c, 1), :] = jnp.sum(chosen, axis=0, keepdims=True)
                after = turned
        return carry

    lax.fori_loop(0, group, step, 0, unroll=4)


def filter_grad(received, local, seqs):
    rows = received.shape[0]
    blocks = rows // seqs
    group = 8
    steps = local // group
    return pl.pallas_call(
        functools.partial(filter_body, local, seqs, group),
        grid=(steps,),
        in_specs=[
            pl.BlockSpec((rows, group, LANES), lambda g: (0, g, 0)),
            pl.BlockSpec((rows, group, LANES), lambda g: (0, steps + g, 0)),
        ],
        out_specs=pl.BlockSpec((blocks, group, LANES), lambda g: (0, g, 0)),
        out_shape=jax.ShapeDtypeStruct((blocks, local, LANES), jnp.float32),
        scratch_shapes=[
            pltpu.VMEM((rows * group, LANES), jnp.float32),
            pltpu.VMEM((rows * group, LANES), jnp.float32),
            pltpu.VMEM((2, 2 * rows, LANES), jnp.float32),
        ],
        compiler_params=params(40),
        cost_estimate=pl.CostEstimate(
            flops=25_000_000_000, bytes_accessed=10_000_000, transcendentals=0
        ),
        name="filter_grad",
    )(received, received)


def finish_body(local, in_ref, grad_ref, value_ref, key_ref, query_out, key_out, value_out):
    same = identity()
    per = LANES // local
    for g in range(grad_ref.shape[1] // LANES):
        at = slice(g * LANES, (g + 1) * LANES)
        block = in_ref[g * per : (g + 1) * per]
        conv = turn(same, block[:, 0].reshape(LANES, LANES))
        back = turn(same, block[:, 1].reshape(LANES, LANES))
        query_out[:, at] = (conv * grad_ref[:, at].astype(jnp.float32)).astype(jnp.bfloat16)
        key_out[:, at] = (back * value_ref[:, at].astype(jnp.float32)).astype(jnp.bfloat16)
        value_out[:, at] = (back * key_ref[:, at].astype(jnp.float32)).astype(jnp.bfloat16)


def finish(received, grad, value, key):
    parts, two, local, lanes = received.shape
    length, channels = key.shape
    width = 2048
    spec = pl.BlockSpec((length, width), lambda g: (0, g))
    shape = jax.ShapeDtypeStruct((length, channels), jnp.bfloat16)
    return pl.pallas_call(
        functools.partial(finish_body, local),
        grid=(channels // width,),
        in_specs=[pl.BlockSpec((width // local, two, local, lanes), lambda g: (g, 0, 0, 0))]
        + [spec] * 3,
        out_specs=(spec,) * 3,
        out_shape=(shape,) * 3,
        compiler_params=params(60),
        cost_estimate=pl.CostEstimate(flops=0, bytes_accessed=20_000_000, transcendentals=0),
        name="finish",
    )(received, grad, value, key)


def exchange(array):
    return lax.all_to_all(array, ("ctx", "dp"), split_axis=0, concat_axis=0, tiled=True)


def spread_lags(lags, seqs):
    me = lax.axis_index("dp")
    held = jnp.zeros_like(lags)
    for offset in range(seqs):
        piece = lax.dynamic_index_in_dim(lags, (me + offset) % seqs, 0, keepdims=True)
        if offset:
            piece = lax.ppermute(piece, "dp", [(s, (s + offset) % seqs) for s in range(seqs)])
        held = lax.dynamic_update_slice_in_dim(held, piece, (me - offset) % seqs, 0)
    return held


def on_device(seqs, blocks, query_act, key_act, value_act, grad_out, filter_taps):
    query, key, value, grad = query_act[0], key_act[0], value_act[0], grad_out[0]
    channels = key.shape[1]
    local = channels // (seqs * blocks)
    share = local // seqs
    received = exchange(send(key, value, grad, query, filter_taps, local, share))
    sums = both(received, local, share, seqs)
    returned = exchange(sums)
    received, sums = lax.optimization_barrier((received, sums))
    lags = filter_grad(received, local, seqs)
    lags = spread_lags(lags.reshape(seqs, blocks // seqs, local, LANES), seqs)
    grad_filter = lags.transpose(1, 3, 0, 2).reshape(blocks // seqs * LANES, seqs * local)
    grad_query, grad_key, grad_value = finish(returned, grad, value, key)
    return (grad_query[None], grad_key[None], grad_value[None], grad_filter)


def solution(mesh):
    seqs, blocks = mesh.shape["dp"], mesh.shape["ctx"]
    spec = P("dp", "ctx", None)
    return jax.shard_map(
        functools.partial(on_device, seqs, blocks),
        mesh=mesh,
        in_specs=(spec, spec, spec, spec, P("ctx", None)),
        out_specs=(spec, spec, spec, P("dp", "ctx")),
        check_vma=False,
    )
```

time: 925 us -> 171 us (0.18); the launches traced: 914 us -> 171 us
  matrix products: 402 us -> 0 us
  local copies, waits for them, and re-layouts: 209 us -> 8.02 us
  other arithmetic: 126 us -> 0 us
  waiting for transfers between devices: 127 us -> 16.4 us
  blocking collectives: 0 us -> 67.5 us
  Pallas kernels: 0 us -> 64.8 us
  starting transfers between devices: 31.7 us -> 13.1 us
  between operations: 14.4 us -> 1.04 us
    dot_general x24 -> x0, matrix products: 402 us -> none  [the longest x12 223 us: apply_second(): jnp.dot(table, flat, precision=lax.Precision.HIGH, preferred_element_type...]
    all_to_all x5 -> x1, waiting for transfers between devices: 126 us -> 0.01 us  [exchange(): lax.all_to_all(array, ('ctx', 'dp'), split_axis=0, concat_axis=0, tiled=T...]
    reshape x6 -> x0, local copies, waits for them, and re-layouts: 71.9 us -> none  [apply_first(): flat = operand.reshape(outer, -1)]
    all_to_all x0 -> x1, blocking collectives: none -> 67.5 us  [exchange(): lax.all_to_all(array, ('ctx', 'dp'), split_axis=0, concat_axis=0, tiled=T...]
    pallas_call x0 -> x4, Pallas kernels: none -> 64.8 us  [the longest x1 27 us: filter_grad(): pl.pallas_call(functools.partial(filter_body, local, seqs, group), grid=(...]
    concatenate x6 -> x0, other arithmetic: 45.5 us -> none  [the longest x2 20.2 us: group_step(): jnp.concatenate([taps_re * prod_re - taps_im * prod_im, taps_re * grad_re...]
    add x2 -> x0, local copies, waits for them, and re-layouts: 32.8 us -> none  [transform(): apply_second(sin_inner, turned_real) + apply_second(cos_inner, turned_imag)]
    sub x2 -> x0, local copies, waits for them, and re-layouts: 32.7 us -> none  [transform(): apply_second(cos_inner, turned_real) - apply_second(sin_inner, turned_imag)]
  transfers between devices with their start and end apart: 6 -> 8, of which waited for: 5 -> 5; matrix products, arithmetic and copies ran while one was open for 6% -> 1% of each run, Pallas kernels for 0% -> 16%
where the time goes in v1:
time: 171 us
  blocking collectives  67.5 us (39%)
  Pallas kernels  64.8 us (38%)
  waiting for transfers between devices  16.4 us (10%)
  starting transfers between devices  13.1 us (8%)
  local copies, waits for them, and re-layouts  8.02 us (5%)
    all_to_all x1, blocking collectives, exchange(): lax.all_to_all(array, ('ctx', 'dp'), split_axis=0, concat_axis=0, tiled=T...  67.5 us
    pallas_call x1, Pallas kernels, filter_grad(): pl.pallas_call(functools.partial(filter_body, local, seqs, group), grid=(...  27 us
    pallas_call x1, Pallas kernels, both(): pl.pallas_call(functools.partial(both_body, local, share, seqs, group), g...  20.2 us
    ppermute x7, waiting for transfers between devices, spread_lags(): lax.ppermute(piece, 'dp', [(s, (s + offset) % seqs) for s in range(seqs)])  16.4 us
    pallas_call x1, Pallas kernels, finish(): pl.pallas_call(functools.partial(finish_body, local), grid=(channels // w...  8.88 us
    pallas_call x1, Pallas kernels, send(): pl.pallas_call(functools.partial(send_body, local, share), grid=(channels...  8.73 us
    unnamed x15, local copies, waits for them, and re-layouts  7.67 us
    ppermute x7, starting transfers between devices, spread_lags(): lax.ppermute(piece, 'dp', [(s, (s + offset) % seqs) for s in range(seqs)])  7.53 us
  transfers between devices with their start and end apart: 8, of which 5 were waited for; matrix products, arithmetic and copies ran while one was open for 1% of the time, Pallas kernels for 16%

profile of v1, /device:TPU:1, one launch (start us, length us, event | category | flops | bytes accessed | tf_op | source)
XLA Modules:
  0.0 170.9 jit_solution(7608201941507944234)
XLA Ops:
  0.6 8.7 %send.1 = bf16[128,136,128]{2,1,0:T(8,128)(2,1)} custom-call(bf16[128,8192]{1,0:T(8,128)(2,1)} %bitcast.17, bf16[128,8192]{1,0:T(8,128)(2,1)} %bitcast.19, bf16[128,8192]{1,0:T(8,128)(2,1)} %bitcast.21, bf16[128,8192]{1,0:T(8,128)(2,1)} %bitcast.25, f32[128,8192]{1,0:T(8,128)} %taps_ref.1), custom_call_target="tpu_custom_call" | custom-call | bytes 20000000 | tf_op jit(solution)/shard_map/send/pallas_call | solution.py:67
  9.4 67.5 %all_to_all.10.prod_ref.grad_ref.taps_ref = bf16[128,136,128]{2,1,0:T(8,128)(2,1)S(1)} all-to-all(bf16[128,136,128]{2,1,0:T(8,128)(2,1)} %send.1), channel_id=1, replica_groups=mesh['dp'=8,'ctx'=16] {'ctx','dp'}, dimensions={0} | all-to-all | bytes 8912896 | tf_op jit(solution)/shard_map/all_to_all | solution.py:272
  76.9 20.2 %both.1 = bf16[128,2,64,128]{3,2,1,0:T(8,128)(2,1)S(1)} custom-call(bf16[128,136,128]{2,1,0:T(8,128)(2,1)S(1)} %all_to_all.10.prod_ref.grad_ref.taps_ref, bf16[128,136,128]{2,1,0:T(8,128)(2,1)S(1)} %all_to_all.10.prod_ref.grad_ref.taps_ref, bf16[128,136,128]{2,1,0:T(8,128)(2,1)S(1)} %all_to_all.10.prod_ref.grad_ref.taps_ref), custom_call_target="tpu_custom_call" | custom-call | flops 20000000000 | bytes 10000000 | tf_op jit(solution)/shard_map/both/pallas_call | solution.py:151
  97.1 2.0 %copy-done = bf16[128,136,128]{2,1,0:T(8,128)(2,1)} copy-done((bf16[128,136,128]{2,1,0:T(8,128)(2,1)}, bf16[128,136,128]{2,1,0:T(8,128)(2,1)S(1)}, u32[]{:S(2)}) %copy-start) | copy-done | bytes 4456472
  99.1 2.0 %copy-done.2 = bf16[128,2,64,128]{3,2,1,0:T(8,128)(2,1)} copy-done((bf16[128,2,64,128]{3,2,1,0:T(8,128)(2,1)}, bf16[128,2,64,128]{3,2,1,0:T(8,128)(2,1)S(1)}, u32[]{:S(2)}) %copy-start.2) | copy-done | bytes 4194328
  101.1 5.5 %all-to-all-start.1 = ((bf16[128,2,64,128]{3,2,1,0:T(8,128)(2,1)}), bf16[128,2,64,128]{3,2,1,0:T(8,128)(2,1)}, u32[]{:S(2)}, u32[]{:S(2)}) async-start(bf16[128,2,64,128]{3,2,1,0:T(8,128)(2,1)} %copy-done.2), calls=%async_computation.1 | async-start | bytes 8388608 | tf_op jit(solution)/shard_map/all_to_all | solution.py:272
  106.9 2.3 %copy-done.1 = bf16[128,136,128]{2,1,0:T(8,128)(2,1)S(1)} copy-done((bf16[128,136,128]{2,1,0:T(8,128)(2,1)S(1)}, bf16[128,136,128]{2,1,0:T(8,128)(2,1)}, u32[]{:S(2)}) %copy-start.1) | copy-done | bytes 4456472
  109.1 27.0 %filter_grad.1 = f32[16,64,128]{2,1,0:T(8,128)S(1)} custom-call(bf16[128,136,128]{2,1,0:T(8,128)(2,1)S(1)} %copy-done.1, bf16[128,136,128]{2,1,0:T(8,128)(2,1)S(1)} %copy-done.1), custom_call_target="tpu_custom_call" | custom-call | flops 24999999488 | bytes 10000000 | tf_op jit(solution)/shard_map/filter_grad/pallas_call | solution.py:217
  136.2 0.1 constant_dynamic-slice_fusion
  136.3 0.1 copy.32
  136.7 1.6 collective-permute-start
  138.3 1.2 collective-permute-start.1
  139.5 1.7 collective-permute-start.2
  141.2 0.5 collective-permute-start.3
  141.7 2.5 %collective-permute-start.4 = (f32[1,2,64,128]{3,1,2,0:T(2,128)S(1)}, f32[1,2,64,128]{3,1,2,0:T(2,128)S(1)}, u32[]{:S(2)}, u32[]{:S(2)}) collective-permute-start(f32[1,2,64,128]{3,1,2,0:T(2,128)S(1)} %copy.31), channel_id=1, source_target_pairs={{0,80},{16,96},{32,112},{48,0},{64,16},{80,32},{96,48},{112,64},{1... | collective-permute-start | bytes 196616 | tf_op jit(solution)/shard_map/ppermute | solution.py:281
  144.2 0.1 broadcast_in_dim.15
  144.3 0.1 copy_dynamic-update-slice_fusion
  144.4 6.0 %collective-permute-done = f32[1,2,64,128]{3,1,2,0:T(2,128)S(1)} collective-permute-done((f32[1,2,64,128]{3,1,2,0:T(2,128)S(1)}, f32[1,2,64,128]{3,1,2,0:T(2,128)S(1)}, u32[]{:S(2)}, u32[]{:S(2)}) %collective-permute-start) | collective-permute-done | bytes 65568 | tf_op jit(solution)/shard_map/ppermute | solution.py:281
  150.4 6.8 %collective-permute-done.1 = f32[1,2,64,128]{3,1,2,0:T(2,128)S(1)} collective-permute-done((f32[1,2,64,128]{3,1,2,0:T(2,128)S(1)}, f32[1,2,64,128]{3,1,2,0:T(2,128)S(1)}, u32[]{:S(2)}, u32[]{:S(2)}) %collective-permute-start.1) | collective-permute-done | bytes 65568 | tf_op jit(solution)/shard_map/ppermute | solution.py:281
  157.3 2.5 %collective-permute-done.3 = f32[1,2,64,128]{3,1,2,0:T(2,128)S(1)} collective-permute-done((f32[1,2,64,128]{3,1,2,0:T(2,128)S(1)}, f32[1,2,64,128]{3,1,2,0:T(2,128)S(1)}, u32[]{:S(2)}, u32[]{:S(2)}) %collective-permute-start.3) | collective-permute-done | bytes 65568 | tf_op jit(solution)/shard_map/ppermute | solution.py:281
  159.8 0.3 collective-permute-done.4
  160.2 0.8 collective-permute-done.6
  161.0 1.0 copy.25
  162.0 8.9 %finish.1 = (bf16[128,8192]{1,0:T(8,128)(2,1)}, bf16[128,8192]{1,0:T(8,128)(2,1)}, bf16[128,8192]{1,0:T(8,128)(2,1)}) custom-call(bf16[128,2,64,128]{3,2,1,0:T(8,128)(2,1)} %all-to-all-done.1.in_ref, bf16[128,8192]{1,0:T(8,128)(2,1)} %bitcast.22, bf16[128,8192]{1,0:T(8,128)(2,1)} %bitcast.20, bf16[128,8192]{1,0:T(8,128)(2,1)} %bitcast.18), custom_call_target="tpu_custom_call" | custom-call | bytes 20000000 | tf_op jit(solution)/shard_map/finish/pallas_call | solution.py:258
  (22 shorter events, 0.5 us)
Async XLA Ops:
  97.1 2.0 %copy-start = (bf16[128,136,128]{2,1,0:T(8,128)(2,1)}, bf16[128,136,128]{2,1,0:T(8,128)(2,1)S(1)}, u32[]{:S(2)}) copy-start(bf16[128,136,128]{2,1,0:T(8,128)(2,1)S(1)} %all_to_all.10.prod_ref.grad_ref.taps_ref) | copy-start | bytes 13369348
  99.1 2.0 %copy-start.2 = (bf16[128,2,64,128]{3,2,1,0:T(8,128)(2,1)}, bf16[128,2,64,128]{3,2,1,0:T(8,128)(2,1)S(1)}, u32[]{:S(2)}) copy-start(bf16[128,2,64,128]{3,2,1,0:T(8,128)(2,1)S(1)} %both.1) | copy-start | bytes 12582916
  101.1 60.9 %all-to-all-start.1 = ((bf16[128,2,64,128]{3,2,1,0:T(8,128)(2,1)}), bf16[128,2,64,128]{3,2,1,0:T(8,128)(2,1)}, u32[]{:S(2)}, u32[]{:S(2)}) async-start(bf16[128,2,64,128]{3,2,1,0:T(8,128)(2,1)} %copy-done.2), calls=%async_computation.1 | async-start | bytes 8388608 | tf_op jit(solution)/shard_map/all_to_all | solution.py:272
  106.9 2.3 %copy-start.1 = (bf16[128,136,128]{2,1,0:T(8,128)(2,1)S(1)}, bf16[128,136,128]{2,1,0:T(8,128)(2,1)}, u32[]{:S(2)}) copy-start(bf16[128,136,128]{2,1,0:T(8,128)(2,1)} %copy-done) | copy-start | bytes 13369348
  136.7 13.7 %collective-permute-start = (f32[1,2,64,128]{3,1,2,0:T(2,128)S(1)}, f32[1,2,64,128]{3,1,2,0:T(2,128)S(1)}, u32[]{:S(2)}, u32[]{:S(2)}) collective-permute-start(f32[1,2,64,128]{3,1,2,0:T(2,128)S(1)} %copy.27), channel_id=1, source_target_pairs={{0,16},{16,32},{32,48},{48,64},{64,80},{80,96},{96,112},{112,0},{1... | collective-permute-start | bytes 196616 | tf_op jit(solution)/shard_map/ppermute | solution.py:281
  138.3 18.9 %collective-permute-start.1 = (f32[1,2,64,128]{3,1,2,0:T(2,128)S(1)}, f32[1,2,64,128]{3,1,2,0:T(2,128)S(1)}, u32[]{:S(2)}, u32[]{:S(2)}) collective-permute-start(f32[1,2,64,128]{3,1,2,0:T(2,128)S(1)} %copy.28), channel_id=1, source_target_pairs={{0,32},{16,48},{32,64},{48,80},{64,96},{80,112},{96,0},{112,16},{1... | collective-permute-start | bytes 196616 | tf_op jit(solution)/shard_map/ppermute | solution.py:281
  139.5 17.8 %collective-permute-start.2 = (f32[1,2,64,128]{3,1,2,0:T(2,128)S(1)}, f32[1,2,64,128]{3,1,2,0:T(2,128)S(1)}, u32[]{:S(2)}, u32[]{:S(2)}) collective-permute-start(f32[1,2,64,128]{3,1,2,0:T(2,128)S(1)} %copy.29), channel_id=1, source_target_pairs={{0,48},{16,64},{32,80},{48,96},{64,112},{80,0},{96,16},{112,32},{1... | collective-permute-start | bytes 196616 | tf_op jit(solution)/shard_map/ppermute | solution.py:281
  141.2 18.6 %collective-permute-start.3 = (f32[1,2,64,128]{3,1,2,0:T(2,128)S(1)}, f32[1,2,64,128]{3,1,2,0:T(2,128)S(1)}, u32[]{:S(2)}, u32[]{:S(2)}) collective-permute-start(f32[1,2,64,128]{3,1,2,0:T(2,128)S(1)} %copy.30), channel_id=1, source_target_pairs={{0,64},{16,80},{32,96},{48,112},{64,0},{80,16},{96,32},{112,48},{1... | collective-permute-start | bytes 196616 | tf_op jit(solution)/shard_map/ppermute | solution.py:281
  141.7 18.4 %collective-permute-start.4 = (f32[1,2,64,128]{3,1,2,0:T(2,128)S(1)}, f32[1,2,64,128]{3,1,2,0:T(2,128)S(1)}, u32[]{:S(2)}, u32[]{:S(2)}) collective-permute-start(f32[1,2,64,128]{3,1,2,0:T(2,128)S(1)} %copy.31), channel_id=1, source_target_pairs={{0,80},{16,96},{32,112},{48,0},{64,16},{80,32},{96,48},{112,64},{1... | collective-permute-start | bytes 196616 | tf_op jit(solution)/shard_map/ppermute | solution.py:281
  150.4 9.7 %collective-permute-start.5 = (f32[1,2,64,128]{3,1,2,0:T(2,128)S(1)}, f32[1,2,64,128]{3,1,2,0:T(2,128)S(1)}, u32[]{:S(2)}, u32[]{:S(2)}) collective-permute-start(f32[1,2,64,128]{3,1,2,0:T(2,128)S(1)} %copy.32), channel_id=1, source_target_pairs={{0,96},{16,112},{32,0},{48,16},{64,32},{80,48},{96,64},{112,80},{1... | collective-permute-start | bytes 196616 | tf_op jit(solution)/shard_map/ppermute | solution.py:281
  157.3 3.7 %collective-permute-start.6 = (f32[1,2,64,128]{3,1,2,0:T(2,128)S(1)}, f32[1,2,64,128]{3,1,2,0:T(2,128)S(1)}, u32[]{:S(2)}, u32[]{:S(2)}) collective-permute-start(f32[1,2,64,128]{3,1,2,0:T(2,128)S(1)} %copy.33), channel_id=1, source_target_pairs={{0,112},{16,0},{32,16},{48,32},{64,48},{80,64},{96,80},{112,96},{1... | collective-permute-start | bytes 196616 | tf_op jit(solution)/shard_map/ppermute | solution.py:281

commit v2 on v1

v2 whole, which is shorter than its diff:
```python
import functools

import jax
import jax.numpy as jnp
from jax import lax
from jax.experimental import pallas as pl
from jax.experimental.pallas import tpu as pltpu
from jax.sharding import PartitionSpec as P

LANES = 128
NT = (((1,), (1,)), ((), ()))


def params(mib):
    return pltpu.CompilerParams(vmem_limit_bytes=mib * 1024 * 1024)


def grid_of(shape):
    return lax.broadcasted_iota(jnp.int32, shape, 0), lax.broadcasted_iota(jnp.int32, shape, 1)


def ones_where(condition):
    return jnp.where(condition, 1.0, 0.0).astype(jnp.bfloat16)


def identity():
    rows, cols = grid_of((LANES, LANES))
    return ones_where(rows == cols)


def reversal():
    rows, cols = grid_of((LANES, LANES))
    return ones_where(rows + cols == LANES - 1)


def turn(matrix, array):
    return lax.dot_general(matrix, array, NT, preferred_element_type=jnp.float32)


def gate(left, right):
    return (left.astype(jnp.float32) * right.astype(jnp.float32)).astype(jnp.bfloat16)


def send_body(local, share, me_ref, key_ref, value_ref, grad_ref, query_ref, low_ref, high_ref, out_ref):
    seqs = out_ref.shape[0]
    per = LANES // local
    same = identity()
    row, lane = grid_of((share, LANES))
    for g in range(key_ref.shape[1] // LANES):
        at = slice(g * LANES, (g + 1) * LANES)
        product = turn(same, gate(key_ref[:, at], value_ref[:, at])).astype(jnp.bfloat16)
        gated = turn(same, gate(grad_ref[:, at], query_ref[:, at])).astype(jnp.bfloat16)
        low, high = low_ref[:, at], high_ref[:, at]
        taps = (
            jnp.where(lane < local, low, pltpu.roll(high, local, 1)),
            jnp.where(lane < local, pltpu.roll(low, local, 1), high),
        )
        for d in range(per):
            x, s = divmod(g * per + d, seqs)
            out_ref[s, x, :local, :] = product[d * local : (d + 1) * local]
            out_ref[s, x, local : 2 * local, :] = gated[d * local : (d + 1) * local]
            out_ref[s, x, 2 * local :, :] = taps[d].astype(jnp.bfloat16)


def send(key, value, grad, query, taps, local, share, seqs):
    length, channels = key.shape
    width = 2048
    message = 2 * local + share
    wide = width // local // seqs
    spec = pl.BlockSpec((length, width), lambda g, me: (0, g))
    return pl.pallas_call(
        functools.partial(send_body, local, share),
        grid_spec=pltpu.PrefetchScalarGridSpec(
            num_scalar_prefetch=1,
            grid=(channels // width,),
            in_specs=[spec] * 4
            + [
                pl.BlockSpec((share, width), lambda g, me: (me[0], g)),
                pl.BlockSpec((share, width), lambda g, me: (seqs + me[0], g)),
            ],
            out_specs=pl.BlockSpec((seqs, wide, message, LANES), lambda g, me: (0, g, 0, 0)),
        ),
        out_shape=jax.ShapeDtypeStruct(
            (seqs, channels // local // seqs, message, LANES), jnp.bfloat16
        ),
        compiler_params=params(60),
        cost_estimate=pl.CostEstimate(flops=0, bytes_accessed=14_000_000, transcendentals=0),
        name="send",
    )(lax.axis_index("dp").astype(jnp.int32).reshape(1), key, value, grad, query, taps, taps)


def rows_of(wide, block, c, seqs, blocks, group):
    return pl.ds(block * group + c, seqs, stride=blocks * group)


def both_body(seqs, blocks, prod_ref, grad_ref, taps_ref, out_ref, prod_wide, grad_wide, taps):
    group = prod_ref.shape[2]
    local = LANES // 2
    share = taps_ref.shape[2]
    flip = reversal()
    g = pl.program_id(0)

    @pl.when(g == 0)
    def _():
        row, lane = grid_of((local, LANES))
        for j in range(0, blocks, 2):
            lags = jnp.concatenate(
                [taps_ref[b, j + side] for side in (0, 1) for b in range(seqs)], axis=0
            )
            lags = lags.astype(jnp.float32).T
            low, high = lags[:local], lags[local:]
            taps[pl.ds(j, local, stride=blocks), :] = jnp.where(
                lane < local, low, pltpu.roll(high, local, 1)
            )
            taps[pl.ds(j + 1, local, stride=blocks), :] = jnp.where(
                lane < local, pltpu.roll(low, local, 1), high
            )

    size = seqs * blocks * group
    prod_wide[...] = prod_ref[...].astype(jnp.float32).reshape(size, LANES)
    grad_wide[...] = jnp.dot(
        grad_ref[...].reshape(size, LANES), flip, preferred_element_type=jnp.float32
    )
    row, lane = grid_of((LANES, LANES))
    same_block = lane >= row
    pairs = blocks // 2

    def step(c, carry):
        def load(wide, block):
            return wide[rows_of(wide, block, c, seqs, blocks, group), :]

        tiles = []
        for i in range(pairs):
            o = pairs - 1 - i
            first = jnp.concatenate([load(prod_wide, 2 * i), load(prod_wide, 2 * i + 1)], axis=1)
            second = jnp.concatenate([load(grad_wide, 2 * o + 1), load(grad_wide, 2 * o)], axis=1)
            tiles.append(jnp.concatenate([first, second], axis=0).astype(jnp.bfloat16))
        lines = jnp.concatenate(tiles, axis=0)
        turned_before = jnp.zeros((LANES, LANES), jnp.float32)
        before = jnp.zeros((LANES, LANES), jnp.bfloat16)
        conv = [None] * pairs
        back = [None] * pairs

        def add(sums, i, piece):
            sums[i] = piece if sums[i] is None else sums[i] + piece

        for k in range(pairs):
            here = []
            for near in (2 * k, 2 * k + 1):
                line = taps[pl.ds((g * group + c) * blocks + near, 1), :]
                turned = pltpu.roll(
                    jnp.broadcast_to(line, (LANES, LANES)), 0, 1, stride=1, stride_axis=0
                )
                here.append(jnp.where(same_block, turned, turned_before).astype(jnp.bfloat16))
                turned_before = turned
            right = jnp.concatenate(
                [
                    jnp.concatenate(here, axis=1),
                    jnp.concatenate([before, here[0]], axis=1),
                ],
                axis=0,
            )
            before = here[1]
            part = jnp.dot(
                lines[: (pairs - k) * 2 * seqs], right, preferred_element_type=jnp.float32
            )
            for i in range(pairs - k):
                at = i * 2 * seqs
                add(conv, i + k, part[at : at + seqs])
                add(back, pairs - 1 - i - k, part[at + seqs : at + 2 * seqs])
        for i in range(pairs):
            for side in (0, 1):
                here = rows_of(prod_wide, 2 * i + side, c, seqs, blocks, group)
                prod_wide[here, :] = conv[i][:, side * LANES : (side + 1) * LANES]
                grad_wide[here, :] = back[i][:, (1 - side) * LANES : (2 - side) * LANES]
        return carry

    lax.fori_loop(0, group, step, 0, unroll=True)
    shape = (seqs, blocks, group, LANES)
    out_ref[:, :, 0] = prod_wide[...].astype(jnp.bfloat16).reshape(shape)
    rounded = grad_wide[...].astype(jnp.bfloat16)
    out_ref[:, :, 1] = (
        jnp.dot(rounded, flip, preferred_element_type=jnp.float32).astype(jnp.bfloat16).reshape(shape)
    )


def both(received, local, share):
    seqs, blocks = received.shape[:2]
    group = 8
    steps = local // group
    size = seqs * blocks * group
    return pl.pallas_call(
        functools.partial(both_body, seqs, blocks),
        grid=(steps,),
        in_specs=[
            pl.BlockSpec((seqs, blocks, group, LANES), lambda g: (0, 0, g, 0)),
            pl.BlockSpec((seqs, blocks, group, LANES), lambda g: (0, 0, steps + g, 0)),
            pl.BlockSpec((seqs, blocks, share, LANES), lambda g: (0, 0, 2 * local // share, 0)),
        ],
        out_specs=pl.BlockSpec((seqs, blocks, 2, group, LANES), lambda g: (0, 0, 0, g, 0)),
        out_shape=jax.ShapeDtypeStruct((seqs, blocks, 2, local, LANES), jnp.bfloat16),
        scratch_shapes=[
            pltpu.VMEM((size, LANES), jnp.float32),
            pltpu.VMEM((size, LANES), jnp.float32),
            pltpu.VMEM((local * blocks, LANES), jnp.float32),
        ],
        compiler_params=params(60),
        cost_estimate=pl.CostEstimate(
            flops=20_000_000_000, bytes_accessed=10_000_000, transcendentals=0
        ),
        name="both",
    )(received, received, received)


def filter_body(seqs, blocks, prod_ref, grad_ref, out_ref, prod_wide, grad_wide):
    group = prod_ref.shape[2]
    size = seqs * blocks * group
    flip = reversal()
    row, lane = grid_of((LANES, LANES))
    same_block = lane <= row
    prod_wide[...] = prod_ref[...].astype(jnp.float32).reshape(size, LANES)
    grad_wide[...] = grad_ref[...].astype(jnp.float32).reshape(size, LANES)
    nothing = jnp.zeros((seqs, LANES), jnp.float32)

    def step(c, carry):
        def load(wide, block):
            return wide[rows_of(wide, block, c, seqs, blocks, group), :]

        prod = jnp.concatenate([load(prod_wide, j) for j in range(blocks)], axis=0)
        lines = turn(flip, prod.astype(jnp.bfloat16)).astype(jnp.bfloat16)
        grad = [load(grad_wide, j) for j in range(blocks)] + [nothing] * 2
        twos = [
            jnp.concatenate([grad[j], grad[j + 1]], axis=0).astype(jnp.bfloat16)
            for j in range(blocks + 1)
        ]

        def shifted(k):
            return jnp.concatenate(
                [twos[min(j + k, blocks)] for j in range(0, blocks, 2)], axis=0
            )

        after = jnp.zeros((LANES, LANES), jnp.float32)
        for k in reversed(range(0, blocks, 2)):
            pair = jnp.concatenate([shifted(k), shifted(k + 1)], axis=1)
            part = jnp.dot(lines, pair, preferred_element_type=jnp.float32)
            for side in (1, 0):
                turned = pltpu.roll(
                    part[:, side * LANES : (side + 1) * LANES], 1, 1, stride=1, stride_axis=0
                )
                chosen = jnp.where(same_block, turned, after)
                out_ref[k + side, pl.ds(c, 1), :] = jnp.sum(chosen, axis=0, keepdims=True)
                after = turned
        return carry

    lax.fori_loop(0, group, step, 0, unroll=4)


def filter_grad(received, local):
    seqs, blocks = received.shape[:2]
    group = 8
    steps = local // group
    size = seqs * blocks * group
    return pl.pallas_call(
        functools.partial(filter_body, seqs, blocks),
        grid=(steps,),
        in_specs=[
            pl.BlockSpec((seqs, blocks, group, LANES), lambda g: (0, 0, g, 0)),
            pl.BlockSpec((seqs, blocks, group, LANES), lambda g: (0, 0, steps + g, 0)),
        ],
        out_specs=pl.BlockSpec((blocks, group, LANES), lambda g: (0, g, 0)),
        out_shape=jax.ShapeDtypeStruct((blocks, local, LANES), jnp.float32),
        scratch_shapes=[pltpu.VMEM((size, LANES), jnp.float32)] * 2,
        compiler_params=params(16),
        cost_estimate=pl.CostEstimate(
            flops=25_000_000_000, bytes_accessed=10_000_000, transcendentals=0
        ),
        name="filter_grad",
    )(received, received)


def finish_body(local, in_ref, grad_ref, value_ref, key_ref, query_out, key_out, value_out):
    same = identity()
    per = LANES // local
    seqs = in_ref.shape[0]
    for g in range(grad_ref.shape[1] // LANES):
        at = slice(g * LANES, (g + 1) * LANES)
        places = [divmod(g * per + d, seqs) for d in range(per)]
        conv = turn(same, jnp.concatenate([in_ref[s, x, 0] for x, s in places], axis=0))
        back = turn(same, jnp.concatenate([in_ref[s, x, 1] for x, s in places], axis=0))
        query_out[:, at] = (conv * grad_ref[:, at].astype(jnp.float32)).astype(jnp.bfloat16)
        key_out[:, at] = (back * value_ref[:, at].astype(jnp.float32)).astype(jnp.bfloat16)
        value_out[:, at] = (back * key_ref[:, at].astype(jnp.float32)).astype(jnp.bfloat16)


def finish(received, grad, value, key):
    seqs, blocks, two, local, lanes = received.shape
    length, channels = key.shape
    width = 2048
    spec = pl.BlockSpec((length, width), lambda g: (0, g))
    shape = jax.ShapeDtypeStruct((length, channels), jnp.bfloat16)
    return pl.pallas_call(
        functools.partial(finish_body, local),
        grid=(channels // width,),
        in_specs=[
            pl.BlockSpec(
                (seqs, width // local // seqs, two, local, lanes), lambda g: (0, g, 0, 0, 0)
            )
        ]
        + [spec] * 3,
        out_specs=(spec,) * 3,
        out_shape=(shape,) * 3,
        compiler_params=params(60),
        cost_estimate=pl.CostEstimate(flops=0, bytes_accessed=20_000_000, transcendentals=0),
        name="finish",
    )(received, grad, value, key)


def exchange(array):
    seqs, blocks, *rest = array.shape
    flat = array.reshape(seqs * blocks, *rest)
    moved = lax.all_to_all(flat, ("dp", "ctx"), split_axis=0, concat_axis=0, tiled=True)
    return moved.reshape(array.shape)


def spread_lags(lags, seqs):
    me = lax.axis_index("dp")
    held = jnp.zeros_like(lags)
    for offset in range(seqs):
        piece = lax.dynamic_index_in_dim(lags, (me + offset) % seqs, 0, keepdims=True)
        if offset:
            piece = lax.ppermute(piece, "dp", [(s, (s + offset) % seqs) for s in range(seqs)])
        held = lax.dynamic_update_slice_in_dim(held, piece, (me - offset) % seqs, 0)
    return held


def on_device(seqs, blocks, query_act, key_act, value_act, grad_out, filter_taps):
    query, key, value, grad = query_act[0], key_act[0], value_act[0], grad_out[0]
    channels = key.shape[1]
    local = channels // (seqs * blocks)
    share = local // seqs
    received = exchange(send(key, value, grad, query, filter_taps, local, share, seqs))
    sums = both(received, local, share)
    returned = exchange(sums)
    received, sums = lax.optimization_barrier((received, sums))
    lags = filter_grad(received, local)
    lags = spread_lags(lags.reshape(seqs, blocks // seqs, local, LANES), seqs)
    grad_filter = lags.transpose(1, 3, 0, 2).reshape(blocks // seqs * LANES, seqs * local)
    grad_query, grad_key, grad_value = finish(returned, grad, value, key)
    return (grad_query[None], grad_key[None], grad_value[None], grad_filter)


def solution(mesh):
    seqs, blocks = mesh.shape["dp"], mesh.shape["ctx"]
    spec = P("dp", "ctx", None)
    return jax.shard_map(
        functools.partial(on_device, seqs, blocks),
        mesh=mesh,
        in_specs=(spec, spec, spec, spec, P("ctx", None)),
        out_specs=(spec, spec, spec, P("dp", "ctx")),
        check_vma=False,
    )
```

time: 171 us -> 172 us (level)
  Pallas kernels: 64.8 us -> 69.5 us
  local copies, waits for them, and re-layouts: 8.02 us -> 4.01 us
  waiting for transfers between devices: 16.4 us -> 12.5 us
  starting transfers between devices: 13.1 us -> 16.8 us
    pallas_call x3, Pallas kernels: 55.9 us -> 60.6 us  [the longest x1 26.6 us: both(): pl.pallas_call(functools.partial(both_body, seqs, blocks), grid=(steps,),...]
    ppermute x7, starting transfers between devices: 7.53 us -> 11.8 us  [spread_lags(): lax.ppermute(piece, 'dp', [(s, (s + offset) % seqs) for s in range(seqs)])]
    unnamed x15 -> x11, local copies, waits for them, and re-layouts: 7.67 us -> 3.66 us
    ppermute x7, waiting for transfers between devices: 16.4 us -> 12.5 us  [spread_lags(): lax.ppermute(piece, 'dp', [(s, (s + offset) % seqs) for s in range(seqs)])]
  transfers between devices with their start and end apart: 8 -> 8, of which waited for: 5 -> 5; matrix products, arithmetic and copies ran while one was open for 1% -> 1% of each run, Pallas kernels for 16% -> 15%
where the time goes in v2:
time: 172 us
  Pallas kernels  69.5 us (40%)
  blocking collectives  68 us (40%)
  starting transfers between devices  16.8 us (10%)
  waiting for transfers between devices  12.5 us (7%)
  local copies, waits for them, and re-layouts  4.01 us (2%)
    all_to_all x1, blocking collectives, exchange(): lax.all_to_all(flat, ('dp', 'ctx'), split_axis=0, concat_axis=0, tiled=True)  68 us
    pallas_call x1, Pallas kernels, both(): pl.pallas_call(functools.partial(both_body, seqs, blocks), grid=(steps,),...  26.6 us
    pallas_call x1, Pallas kernels, filter_grad(): pl.pallas_call(functools.partial(filter_body, seqs, blocks), grid=(steps,...  26.5 us
    ppermute x7, waiting for transfers between devices, spread_lags(): lax.ppermute(piece, 'dp', [(s, (s + offset) % seqs) for s in range(seqs)])  12.5 us
    ppermute x7, starting transfers between devices, spread_lags(): lax.ppermute(piece, 'dp', [(s, (s + offset) % seqs) for s in range(seqs)])  11.8 us
    pallas_call x1, Pallas kernels, finish(): pl.pallas_call(functools.partial(finish_body, local), grid=(channels // w...  8.86 us
    pallas_call x1, Pallas kernels, send(): pl.pallas_call(functools.partial(send_body, local, share), grid_spec=pltp...  7.53 us
    all_to_all x1, starting transfers between devices, exchange(): lax.all_to_all(flat, ('dp', 'ctx'), split_axis=0, concat_axis=0, tiled=True)  5.03 us
  transfers between devices with their start and end apart: 8, of which 5 were waited for; matrix products, arithmetic and copies ran while one was open for 1% of the time, Pallas kernels for 15%

profile of v2, /device:TPU:1, one launch (start us, length us, event | category | flops | bytes accessed | tf_op | source)
XLA Modules:
  0.0 171.9 jit_solution(16374203378340534904)
XLA Ops:
  0.6 7.5 %send.1 = bf16[8,16,136,128]{3,2,1,0:T(8,128)(2,1)} custom-call(s32[1]{0:T(128)} %bitcast.me_ref, bf16[128,8192]{1,0:T(8,128)(2,1)} %bitcast.28, bf16[128,8192]{1,0:T(8,128)(2,1)} %bitcast.30, bf16[128,8192]{1,0:T(8,128)(2,1)} %bitcast.32, bf16[128,8192]{1,0:T(8,128)(2,1)} %bitcast.35, f32[128,8192]{1,0:T(8,128)} %high_ref.1, f32[128,8192]{1,0:T(8,128)} %high_ref.1), custom_call_target="tpu_custom_call" | custom-call | bytes 14000000 | tf_op jit(solution)/shard_map/send/pallas_call | solution.py:71
  8.2 68.0 %all_to_all.10 = bf16[128,136,128]{2,1,0:T(8,128)(2,1)} all-to-all(bf16[128,136,128]{2,1,0:T(8,128)(2,1)} %bitcast.27), channel_id=1, replica_groups=mesh['dp'=8,'ctx'=16] {'dp','ctx'}, dimensions={0} | all-to-all | bytes 8912896 | tf_op jit(solution)/shard_map/all_to_all | solution.py:321
  76.2 26.6 %both.1 = bf16[8,16,2,64,128]{4,3,2,1,0:T(8,128)(2,1)} custom-call(bf16[8,16,136,128]{3,2,1,0:T(8,128)(2,1)} %bitcast.21, bf16[8,16,136,128]{3,2,1,0:T(8,128)(2,1)} %bitcast.22, bf16[8,16,136,128]{3,2,1,0:T(8,128)(2,1)} %bitcast.23), custom_call_target="tpu_custom_call" | custom-call | flops 20000000000 | bytes 10000000 | tf_op jit(solution)/shard_map/both/pallas_call | solution.py:192
  102.8 5.0 %all-to-all-start.1 = ((bf16[128,2,64,128]{3,2,1,0:T(8,128)(2,1)}), bf16[128,2,64,128]{3,2,1,0:T(8,128)(2,1)}, u32[]{:S(2)}, u32[]{:S(2)}) async-start(bf16[128,2,64,128]{3,2,1,0:T(8,128)(2,1)} %bitcast.34), calls=%async_computation.1 | async-start | bytes 8388608 | tf_op jit(solution)/shard_map/all_to_all | solution.py:321
  108.1 2.3 %copy-done = bf16[128,136,128]{2,1,0:T(8,128)(2,1)S(1)} copy-done((bf16[128,136,128]{2,1,0:T(8,128)(2,1)S(1)}, bf16[128,136,128]{2,1,0:T(8,128)(2,1)}, u32[]{:S(2)}) %copy-start) | copy-done | bytes 4456472
  110.3 26.5 %filter_grad.1 = f32[16,64,128]{2,1,0:T(8,128)S(1)} custom-call(bf16[8,16,136,128]{3,2,1,0:T(8,128)(2,1)S(1)} %bitcast.24, bf16[8,16,136,128]{3,2,1,0:T(8,128)(2,1)S(1)} %bitcast.25), custom_call_target="tpu_custom_call" | custom-call | flops 24999999488 | bytes 10000000 | tf_op jit(solution)/shard_map/filter_grad/pallas_call | solution.py:263
  136.8 0.1 constant_dynamic-slice_fusion
  137.0 0.1 copy.32
  137.0 0.1 copy.31
  137.3 1.7 collective-permute-start
  139.0 1.2 collective-permute-start.1
  140.3 1.7 collective-permute-start.2
  142.0 0.4 collective-permute-start.3
  142.4 2.6 %collective-permute-start.4 = (f32[1,2,64,128]{3,1,2,0:T(2,128)S(1)}, f32[1,2,64,128]{3,1,2,0:T(2,128)S(1)}, u32[]{:S(2)}, u32[]{:S(2)}) collective-permute-start(f32[1,2,64,128]{3,1,2,0:T(2,128)S(1)} %copy.31), channel_id=1, source_target_pairs={{0,80},{16,96},{32,112},{48,0},{64,16},{80,32},{96,48},{112,64},{1... | collective-permute-start | bytes 196616 | tf_op jit(solution)/shard_map/ppermute | solution.py:331
  145.0 0.1 broadcast_in_dim.15
  145.1 0.1 copy_dynamic-update-slice_fusion
  145.2 4.1 %collective-permute-start.5 = (f32[1,2,64,128]{3,1,2,0:T(2,128)S(1)}, f32[1,2,64,128]{3,1,2,0:T(2,128)S(1)}, u32[]{:S(2)}, u32[]{:S(2)}) collective-permute-start(f32[1,2,64,128]{3,1,2,0:T(2,128)S(1)} %copy.32), channel_id=1, source_target_pairs={{0,96},{16,112},{32,0},{48,16},{64,32},{80,48},{96,64},{112,80},{1... | collective-permute-start | bytes 196616 | tf_op jit(solution)/shard_map/ppermute | solution.py:331
  149.4 8.9 %collective-permute-done.1 = f32[1,2,64,128]{3,1,2,0:T(2,128)S(1)} collective-permute-done((f32[1,2,64,128]{3,1,2,0:T(2,128)S(1)}, f32[1,2,64,128]{3,1,2,0:T(2,128)S(1)}, u32[]{:S(2)}, u32[]{:S(2)}) %collective-permute-start.1) | collective-permute-done | bytes 65568 | tf_op jit(solution)/shard_map/ppermute | solution.py:331
  158.3 0.5 collective-permute-done.2
  158.8 2.0 %collective-permute-done.3 = f32[1,2,64,128]{3,1,2,0:T(2,128)S(1)} collective-permute-done((f32[1,2,64,128]{3,1,2,0:T(2,128)S(1)}, f32[1,2,64,128]{3,1,2,0:T(2,128)S(1)}, u32[]{:S(2)}, u32[]{:S(2)}) %collective-permute-start.3) | collective-permute-done | bytes 65568 | tf_op jit(solution)/shard_map/ppermute | solution.py:331
  160.8 0.5 collective-permute-done.4
  161.3 0.6 collective-permute-done.6
  162.0 1.0 copy.25
  163.0 8.9 %finish.1 = (bf16[128,8192]{1,0:T(8,128)(2,1)}, bf16[128,8192]{1,0:T(8,128)(2,1)}, bf16[128,8192]{1,0:T(8,128)(2,1)}) custom-call(bf16[8,16,2,64,128]{4,3,2,1,0:T(8,128)(2,1)} %bitcast.8.in_ref, bf16[128,8192]{1,0:T(8,128)(2,1)} %bitcast.33, bf16[128,8192]{1,0:T(8,128)(2,1)} %bitcast.31, bf16[128,8192]{1,0:T(8,128)(2,1)} %bitcast.29), custom_call_target="tpu_custom_call" | custom-call | bytes 20000000 | tf_op jit(solution)/shard_map/finish/pallas_call | solution.py:301
  (18 shorter events, 0.4 us)
Async XLA Ops:
  102.8 60.3 %all-to-all-start.1 = ((bf16[128,2,64,128]{3,2,1,0:T(8,128)(2,1)}), bf16[128,2,64,128]{3,2,1,0:T(8,128)(2,1)}, u32[]{:S(2)}, u32[]{:S(2)}) async-start(bf16[128,2,64,128]{3,2,1,0:T(8,128)(2,1)} %bitcast.34), calls=%async_computation.1 | async-start | bytes 8388608 | tf_op jit(solution)/shard_map/all_to_all | solution.py:321
  108.1 2.3 %copy-start = (bf16[128,136,128]{2,1,0:T(8,128)(2,1)S(1)}, bf16[128,136,128]{2,1,0:T(8,128)(2,1)}, u32[]{:S(2)}) copy-start(bf16[128,136,128]{2,1,0:T(8,128)(2,1)} %all_to_all.10) | copy-start | bytes 13369348
  137.3 7.9 %collective-permute-start = (f32[1,2,64,128]{3,1,2,0:T(2,128)S(1)}, f32[1,2,64,128]{3,1,2,0:T(2,128)S(1)}, u32[]{:S(2)}, u32[]{:S(2)}) collective-permute-start(f32[1,2,64,128]{3,1,2,0:T(2,128)S(1)} %copy.27), channel_id=1, source_target_pairs={{0,16},{16,32},{32,48},{48,64},{64,80},{80,96},{96,112},{112,0},{1... | collective-permute-start | bytes 196616 | tf_op jit(solution)/shard_map/ppermute | solution.py:331
  139.0 19.3 %collective-permute-start.1 = (f32[1,2,64,128]{3,1,2,0:T(2,128)S(1)}, f32[1,2,64,128]{3,1,2,0:T(2,128)S(1)}, u32[]{:S(2)}, u32[]{:S(2)}) collective-permute-start(f32[1,2,64,128]{3,1,2,0:T(2,128)S(1)} %copy.28), channel_id=1, source_target_pairs={{0,32},{16,48},{32,64},{48,80},{64,96},{80,112},{96,0},{112,16},{1... | collective-permute-start | bytes 196616 | tf_op jit(solution)/shard_map/ppermute | solution.py:331
  140.3 18.5 %collective-permute-start.2 = (f32[1,2,64,128]{3,1,2,0:T(2,128)S(1)}, f32[1,2,64,128]{3,1,2,0:T(2,128)S(1)}, u32[]{:S(2)}, u32[]{:S(2)}) collective-permute-start(f32[1,2,64,128]{3,1,2,0:T(2,128)S(1)} %copy.29), channel_id=1, source_target_pairs={{0,48},{16,64},{32,80},{48,96},{64,112},{80,0},{96,16},{112,32},{1... | collective-permute-start | bytes 196616 | tf_op jit(solution)/shard_map/ppermute | solution.py:331
  142.0 18.8 %collective-permute-start.3 = (f32[1,2,64,128]{3,1,2,0:T(2,128)S(1)}, f32[1,2,64,128]{3,1,2,0:T(2,128)S(1)}, u32[]{:S(2)}, u32[]{:S(2)}) collective-permute-start(f32[1,2,64,128]{3,1,2,0:T(2,128)S(1)} %copy.30), channel_id=1, source_target_pairs={{0,64},{16,80},{32,96},{48,112},{64,0},{80,16},{96,32},{112,48},{1... | collective-permute-start | bytes 196616 | tf_op jit(solution)/shard_map/ppermute | solution.py:331
  142.4 18.9 %collective-permute-start.4 = (f32[1,2,64,128]{3,1,2,0:T(2,128)S(1)}, f32[1,2,64,128]{3,1,2,0:T(2,128)S(1)}, u32[]{:S(2)}, u32[]{:S(2)}) collective-permute-start(f32[1,2,64,128]{3,1,2,0:T(2,128)S(1)} %copy.31), channel_id=1, source_target_pairs={{0,80},{16,96},{32,112},{48,0},{64,16},{80,32},{96,48},{112,64},{1... | collective-permute-start | bytes 196616 | tf_op jit(solution)/shard_map/ppermute | solution.py:331
  145.2 16.1 %collective-permute-start.5 = (f32[1,2,64,128]{3,1,2,0:T(2,128)S(1)}, f32[1,2,64,128]{3,1,2,0:T(2,128)S(1)}, u32[]{:S(2)}, u32[]{:S(2)}) collective-permute-start(f32[1,2,64,128]{3,1,2,0:T(2,128)S(1)} %copy.32), channel_id=1, source_target_pairs={{0,96},{16,112},{32,0},{48,16},{64,32},{80,48},{96,64},{112,80},{1... | collective-permute-start | bytes 196616 | tf_op jit(solution)/shard_map/ppermute | solution.py:331
  158.3 3.7 %collective-permute-start.6 = (f32[1,2,64,128]{3,1,2,0:T(2,128)S(1)}, f32[1,2,64,128]{3,1,2,0:T(2,128)S(1)}, u32[]{:S(2)}, u32[]{:S(2)}) collective-permute-start(f32[1,2,64,128]{3,1,2,0:T(2,128)S(1)} %copy.33), channel_id=1, source_target_pairs={{0,112},{16,0},{32,16},{48,32},{64,48},{80,64},{96,80},{112,96},{1... | collective-permute-start | bytes 196616 | tf_op jit(solution)/shard_map/ppermute | solution.py:331

commit v3 on v2

--- a/solution.py
+++ b/solution.py
@@ -44,12 +44,15 @@
 def send_body(local, share, me_ref, key_ref, value_ref, grad_ref, query_ref, low_ref, high_ref, out_ref):
     seqs = out_ref.shape[0]
     per = LANES // local
-    same = identity()
+    flip = reversal()
     row, lane = grid_of((share, LANES))
     for g in range(key_ref.shape[1] // LANES):
         at = slice(g * LANES, (g + 1) * LANES)
-        product = turn(same, gate(key_ref[:, at], value_ref[:, at])).astype(jnp.bfloat16)
-        gated = turn(same, gate(grad_ref[:, at], query_ref[:, at])).astype(jnp.bfloat16)
+        product = gate(key_ref[:, at], value_ref[:, at]).T
+        gated = jnp.dot(
+            flip, gate(grad_ref[:, at], query_ref[:, at]), preferred_element_type=jnp.float32
+        )
+        gated = gated.astype(jnp.bfloat16).T
         low, high = low_ref[:, at], high_ref[:, at]
         taps = (
             jnp.where(lane < local, low, pltpu.roll(high, local, 1)),
@@ -64,7 +67,7 @@
 
 def send(key, value, grad, query, taps, local, share, seqs):
     length, channels = key.shape
-    width = 2048
+    width = 4096
     message = 2 * local + share
     wide = width // local // seqs
     spec = pl.BlockSpec((length, width), lambda g, me: (0, g))
@@ -90,14 +93,12 @@
 
 
 def rows_of(wide, block, c, seqs, blocks, group):
-    return pl.ds(block * group + c, seqs, stride=blocks * group)
+    return pl.ds(block * seqs * group + c, seqs, stride=group)
 
 
 def both_body(seqs, blocks, prod_ref, grad_ref, taps_ref, out_ref, prod_wide, grad_wide, taps):
     group = prod_ref.shape[2]
     local = LANES // 2
-    share = taps_ref.shape[2]
-    flip = reversal()
     g = pl.program_id(0)
 
     @pl.when(g == 0)
@@ -116,11 +117,11 @@
                 lane < local, pltpu.roll(low, local, 1), high
             )
 
-    size = seqs * blocks * group
-    prod_wide[...] = prod_ref[...].astype(jnp.float32).reshape(size, LANES)
-    grad_wide[...] = jnp.dot(
-        grad_ref[...].reshape(size, LANES), flip, preferred_element_type=jnp.float32
-    )
+    for b in range(seqs):
+        for j in range(blocks):
+            at = slice((j * seqs + b) * group, (j * seqs + b + 1) * group)
+            prod_wide[at, :] = prod_ref[b, j].astype(jnp.float32)
+            grad_wide[at, :] = grad_ref[b, j].astype(jnp.float32)
     row, lane = grid_of((LANES, LANES))
     same_block = lane >= row
     pairs = blocks // 2
@@ -176,12 +177,11 @@
         return carry
 
     lax.fori_loop(0, group, step, 0, unroll=True)
-    shape = (seqs, blocks, group, LANES)
-    out_ref[:, :, 0] = prod_wide[...].astype(jnp.bfloat16).reshape(shape)
-    rounded = grad_wide[...].astype(jnp.bfloat16)
-    out_ref[:, :, 1] = (
-        jnp.dot(rounded, flip, preferred_element_type=jnp.float32).astype(jnp.bfloat16).reshape(shape)
-    )
+    for b in range(seqs):
+        for j in range(blocks):
+            at = slice((j * seqs + b) * group, (j * seqs + b + 1) * group)
+            out_ref[b, j, 0] = prod_wide[at, :].astype(jnp.bfloat16)
+            out_ref[b, j, 1] = grad_wide[at, :].astype(jnp.bfloat16)
 
 
 def both(received, local, share):
@@ -212,14 +212,16 @@
     )(received, received, received)
 
 
-def filter_body(seqs, blocks, prod_ref, grad_ref, out_ref, prod_wide, grad_wide):
+def filter_body(seqs, blocks, prod_ref, grad_ref, out_ref, prod_wide, grad_wide, found):
     group = prod_ref.shape[2]
-    size = seqs * blocks * group
-    flip = reversal()
+    same = identity()
     row, lane = grid_of((LANES, LANES))
-    same_block = lane <= row
-    prod_wide[...] = prod_ref[...].astype(jnp.float32).reshape(size, LANES)
-    grad_wide[...] = grad_ref[...].astype(jnp.float32).reshape(size, LANES)
+    same_block = lane >= row
+    for b in range(seqs):
+        for j in range(blocks):
+            at = slice((j * seqs + b) * group, (j * seqs + b + 1) * group)
+            prod_wide[at, :] = prod_ref[b, j].astype(jnp.float32)
+            grad_wide[at, :] = grad_ref[b, j].astype(jnp.float32)
     nothing = jnp.zeros((seqs, LANES), jnp.float32)
 
     def step(c, carry):
@@ -227,7 +229,7 @@
             return wide[rows_of(wide, block, c, seqs, blocks, group), :]
 
         prod = jnp.concatenate([load(prod_wide, j) for j in range(blocks)], axis=0)
-        lines = turn(flip, prod.astype(jnp.bfloat16)).astype(jnp.bfloat16)
+        lines = turn(same, prod.astype(jnp.bfloat16)).astype(jnp.bfloat16)
         grad = [load(grad_wide, j) for j in range(blocks)] + [nothing] * 2
         twos = [
             jnp.concatenate([grad[j], grad[j + 1]], axis=0).astype(jnp.bfloat16)
@@ -245,14 +247,20 @@
             part = jnp.dot(lines, pair, preferred_element_type=jnp.float32)
             for side in (1, 0):
                 turned = pltpu.roll(
-                    part[:, side * LANES : (side + 1) * LANES], 1, 1, stride=1, stride_axis=0
+                    part[:, side * LANES : (side + 1) * LANES], 0, 1, stride=1, stride_axis=0
                 )
                 chosen = jnp.where(same_block, turned, after)
-                out_ref[k + side, pl.ds(c, 1), :] = jnp.sum(chosen, axis=0, keepdims=True)
+                found[pl.ds((k + side) * group + c, 1), :] = jnp.sum(chosen, axis=0, keepdims=True)
                 after = turned
         return carry
 
     lax.fori_loop(0, group, step, 0, unroll=4)
+    rows, cols = grid_of((LANES, LANES))
+    flip = jnp.where(rows + cols == LANES - 1, 1.0, 0.0)
+    lags = jnp.dot(
+        found[...], flip, precision=lax.Precision.HIGHEST, preferred_element_type=jnp.float32
+    )
+    out_ref[...] = lags.reshape(blocks, group, LANES)
 
 
 def filter_grad(received, local):
@@ -269,7 +277,8 @@
         ],
         out_specs=pl.BlockSpec((blocks, group, LANES), lambda g: (0, g, 0)),
         out_shape=jax.ShapeDtypeStruct((blocks, local, LANES), jnp.float32),
-        scratch_shapes=[pltpu.VMEM((size, LANES), jnp.float32)] * 2,
+        scratch_shapes=[pltpu.VMEM((size, LANES), jnp.float32)] * 2
+        + [pltpu.VMEM((blocks * group, LANES), jnp.float32)],
         compiler_params=params(16),
         cost_estimate=pl.CostEstimate(
             flops=25_000_000_000, bytes_accessed=10_000_000, transcendentals=0
@@ -279,14 +288,16 @@
 
 
 def finish_body(local, in_ref, grad_ref, value_ref, key_ref, query_out, key_out, value_out):
-    same = identity()
+    flip = reversal()
     per = LANES // local
     seqs = in_ref.shape[0]
     for g in range(grad_ref.shape[1] // LANES):
         at = slice(g * LANES, (g + 1) * LANES)
         places = [divmod(g * per + d, seqs) for d in range(per)]
-        conv = turn(same, jnp.concatenate([in_ref[s, x, 0] for x, s in places], axis=0))
-        back = turn(same, jnp.concatenate([in_ref[s, x, 1] for x, s in places], axis=0))
+        conv = jnp.concatenate([in_ref[s, x, 0] for x, s in places], axis=0).T
+        conv = conv.astype(jnp.float32)
+        back = jnp.concatenate([in_ref[s, x, 1] for x, s in places], axis=0).T
+        back = jnp.dot(flip, back, preferred_element_type=jnp.float32)
         query_out[:, at] = (conv * grad_ref[:, at].astype(jnp.float32)).astype(jnp.bfloat16)
         key_out[:, at] = (back * value_ref[:, at].astype(jnp.float32)).astype(jnp.bfloat16)
         value_out[:, at] = (back * key_ref[:, at].astype(jnp.float32)).astype(jnp.bfloat16)
@@ -295,7 +306,7 @@
 def finish(received, grad, value, key):
     seqs, blocks, two, local, lanes = received.shape
     length, channels = key.shape
-    width = 2048
+    width = 4096
     spec = pl.BlockSpec((length, width), lambda g: (0, g))
     shape = jax.ShapeDtypeStruct((length, channels), jnp.bfloat16)
     return pl.pallas_call(

time: 172 us -> 159 us (0.924)
  Pallas kernels: 69.5 us -> 58.1 us
  starting transfers between devices: 16.8 us -> 14.7 us
    pallas_call x1, Pallas kernels: 26.6 us -> 17 us  [both(): pl.pallas_call(functools.partial(both_body, seqs, blocks), grid=(steps,),...]
    pallas_call x1, Pallas kernels: 26.5 us -> 28.7 us  [filter_grad(): pl.pallas_call(functools.partial(filter_body, seqs, blocks), grid=(steps,...]
    ppermute x7, starting transfers between devices: 11.8 us -> 9.66 us  [spread_lags(): lax.ppermute(piece, 'dp', [(s, (s + offset) % seqs) for s in range(seqs)])]
    pallas_call x1, Pallas kernels: 8.86 us -> 6.71 us  [finish(): pl.pallas_call(functools.partial(finish_body, local), grid=(channels // w...]
    pallas_call x1, Pallas kernels: 7.53 us -> 5.76 us  [send(): pl.pallas_call(functools.partial(send_body, local, share), grid_spec=pltp...]
  transfers between devices with their start and end apart: 8 -> 8, of which waited for: 5 -> 5; matrix products, arithmetic and copies ran while one was open for 1% -> 1% of each run, Pallas kernels for 15% -> 18%
where the time goes in v3:
time: 159 us; the launch traced here: 158 us
  blocking collectives  68 us (43%)
  Pallas kernels  58.1 us (37%)
  starting transfers between devices  14.7 us (9%)
  waiting for transfers between devices  12.5 us (8%)
  local copies, waits for them, and re-layouts  4.01 us (3%)
    all_to_all x1, blocking collectives, exchange(): lax.all_to_all(flat, ('dp', 'ctx'), split_axis=0, concat_axis=0, tiled=True)  68 us
    pallas_call x1, Pallas kernels, filter_grad(): pl.pallas_call(functools.partial(filter_body, seqs, blocks), grid=(steps,...  28.7 us
    pallas_call x1, Pallas kernels, both(): pl.pallas_call(functools.partial(both_body, seqs, blocks), grid=(steps,),...  17 us
    ppermute x7, waiting for transfers between devices, spread_lags(): lax.ppermute(piece, 'dp', [(s, (s + offset) % seqs) for s in range(seqs)])  12.5 us
    ppermute x7, starting transfers between devices, spread_lags(): lax.ppermute(piece, 'dp', [(s, (s + offset) % seqs) for s in range(seqs)])  9.66 us
    pallas_call x1, Pallas kernels, finish(): pl.pallas_call(functools.partial(finish_body, local), grid=(channels // w...  6.71 us
    pallas_call x1, Pallas kernels, send(): pl.pallas_call(functools.partial(send_body, local, share), grid_spec=pltp...  5.76 us
    all_to_all x1, starting transfers between devices, exchange(): lax.all_to_all(flat, ('dp', 'ctx'), split_axis=0, concat_axis=0, tiled=True)  5.03 us
  transfers between devices with their start and end apart: 8, of which 5 were waited for; matrix products, arithmetic and copies ran while one was open for 1% of the time, Pallas kernels for 18%

profile of v3, /device:TPU:1, one launch (start us, length us, event | category | flops | bytes accessed | tf_op | source)
XLA Modules:
  0.0 158.4 jit_solution(13051678852702951703)
XLA Ops:
  0.6 5.8 %send.1 = bf16[8,16,136,128]{3,2,1,0:T(8,128)(2,1)} custom-call(s32[1]{0:T(128)} %bitcast.me_ref, bf16[128,8192]{1,0:T(8,128)(2,1)} %bitcast.28, bf16[128,8192]{1,0:T(8,128)(2,1)} %bitcast.30, bf16[128,8192]{1,0:T(8,128)(2,1)} %bitcast.32, bf16[128,8192]{1,0:T(8,128)(2,1)} %bitcast.35, f32[128,8192]{1,0:T(8,128)} %high_ref.1, f32[128,8192]{1,0:T(8,128)} %high_ref.1), custom_call_target="tpu_custom_call" | custom-call | bytes 14000000 | tf_op jit(solution)/shard_map/send/pallas_call | solution.py:74
  6.4 68.0 %all_to_all.10 = bf16[128,136,128]{2,1,0:T(8,128)(2,1)} all-to-all(bf16[128,136,128]{2,1,0:T(8,128)(2,1)} %bitcast.27), channel_id=1, replica_groups=mesh['dp'=8,'ctx'=16] {'dp','ctx'}, dimensions={0} | all-to-all | bytes 8912896 | tf_op jit(solution)/shard_map/all_to_all | solution.py:332
  74.4 17.0 %both.1 = bf16[8,16,2,64,128]{4,3,2,1,0:T(8,128)(2,1)} custom-call(bf16[8,16,136,128]{3,2,1,0:T(8,128)(2,1)} %bitcast.21, bf16[8,16,136,128]{3,2,1,0:T(8,128)(2,1)} %bitcast.22, bf16[8,16,136,128]{3,2,1,0:T(8,128)(2,1)} %bitcast.23), custom_call_target="tpu_custom_call" | custom-call | flops 20000000000 | bytes 10000000 | tf_op jit(solution)/shard_map/both/pallas_call | solution.py:192
  91.4 5.0 %all-to-all-start.1 = ((bf16[128,2,64,128]{3,2,1,0:T(8,128)(2,1)}), bf16[128,2,64,128]{3,2,1,0:T(8,128)(2,1)}, u32[]{:S(2)}, u32[]{:S(2)}) async-start(bf16[128,2,64,128]{3,2,1,0:T(8,128)(2,1)} %bitcast.34), calls=%async_computation.1 | async-start | bytes 8388608 | tf_op jit(solution)/shard_map/all_to_all | solution.py:332
  96.7 2.3 %copy-done = bf16[128,136,128]{2,1,0:T(8,128)(2,1)S(1)} copy-done((bf16[128,136,128]{2,1,0:T(8,128)(2,1)S(1)}, bf16[128,136,128]{2,1,0:T(8,128)(2,1)}, u32[]{:S(2)}) %copy-start) | copy-done | bytes 4456472
  99.0 28.7 %filter_grad.1 = f32[16,64,128]{2,1,0:T(8,128)S(1)} custom-call(bf16[8,16,136,128]{3,2,1,0:T(8,128)(2,1)S(1)} %bitcast.24, bf16[8,16,136,128]{3,2,1,0:T(8,128)(2,1)S(1)} %bitcast.25), custom_call_target="tpu_custom_call" | custom-call | flops 24999999488 | bytes 10000000 | tf_op jit(solution)/shard_map/filter_grad/pallas_call | solution.py:271
  127.6 0.1 constant_dynamic-slice_fusion
  127.7 0.1 copy.33
  127.7 0.1 copy.32
  128.1 1.7 %collective-permute-start = (f32[1,2,64,128]{3,1,2,0:T(2,128)S(1)}, f32[1,2,64,128]{3,1,2,0:T(2,128)S(1)}, u32[]{:S(2)}, u32[]{:S(2)}) collective-permute-start(f32[1,2,64,128]{3,1,2,0:T(2,128)S(1)} %copy.27), channel_id=1, source_target_pairs={{0,16},{16,32},{32,48},{48,64},{64,80},{80,96},{96,112},{112,0},{1... | collective-permute-start | bytes 196616 | tf_op jit(solution)/shard_map/ppermute | solution.py:342
  129.8 1.2 collective-permute-start.1
  131.0 1.7 %collective-permute-start.2 = (f32[1,2,64,128]{3,1,2,0:T(2,128)S(1)}, f32[1,2,64,128]{3,1,2,0:T(2,128)S(1)}, u32[]{:S(2)}, u32[]{:S(2)}) collective-permute-start(f32[1,2,64,128]{3,1,2,0:T(2,128)S(1)} %copy.29), channel_id=1, source_target_pairs={{0,48},{16,64},{32,80},{48,96},{64,112},{80,0},{96,16},{112,32},{1... | collective-permute-start | bytes 196616 | tf_op jit(solution)/shard_map/ppermute | solution.py:342
  132.8 0.4 collective-permute-start.3
  133.2 2.6 %collective-permute-start.4 = (f32[1,2,64,128]{3,1,2,0:T(2,128)S(1)}, f32[1,2,64,128]{3,1,2,0:T(2,128)S(1)}, u32[]{:S(2)}, u32[]{:S(2)}) collective-permute-start(f32[1,2,64,128]{3,1,2,0:T(2,128)S(1)} %copy.31), channel_id=1, source_target_pairs={{0,80},{16,96},{32,112},{48,0},{64,16},{80,32},{96,48},{112,64},{1... | collective-permute-start | bytes 196616 | tf_op jit(solution)/shard_map/ppermute | solution.py:342
  135.8 0.1 broadcast_in_dim.15
  135.9 0.1 copy_dynamic-update-slice_fusion
  136.0 2.0 %collective-permute-start.5 = (f32[1,2,64,128]{3,1,2,0:T(2,128)S(1)}, f32[1,2,64,128]{3,1,2,0:T(2,128)S(1)}, u32[]{:S(2)}, u32[]{:S(2)}) collective-permute-start(f32[1,2,64,128]{3,1,2,0:T(2,128)S(1)} %copy.32), channel_id=1, source_target_pairs={{0,96},{16,112},{32,0},{48,16},{64,32},{80,48},{96,64},{112,80},{1... | collective-permute-start | bytes 196616 | tf_op jit(solution)/shard_map/ppermute | solution.py:342
  138.0 8.9 %collective-permute-done.1 = f32[1,2,64,128]{3,1,2,0:T(2,128)S(1)} collective-permute-done((f32[1,2,64,128]{3,1,2,0:T(2,128)S(1)}, f32[1,2,64,128]{3,1,2,0:T(2,128)S(1)}, u32[]{:S(2)}, u32[]{:S(2)}) %collective-permute-start.1) | collective-permute-done | bytes 65568 | tf_op jit(solution)/shard_map/ppermute | solution.py:342
  146.9 0.5 collective-permute-done.2
  147.4 2.0 %collective-permute-done.3 = f32[1,2,64,128]{3,1,2,0:T(2,128)S(1)} collective-permute-done((f32[1,2,64,128]{3,1,2,0:T(2,128)S(1)}, f32[1,2,64,128]{3,1,2,0:T(2,128)S(1)}, u32[]{:S(2)}, u32[]{:S(2)}) %collective-permute-start.3) | collective-permute-done | bytes 65568 | tf_op jit(solution)/shard_map/ppermute | solution.py:342
  149.4 0.5 collective-permute-done.4
  150.0 0.6 collective-permute-done.6
  150.7 1.0 copy.25
  151.7 6.7 %finish.1 = (bf16[128,8192]{1,0:T(8,128)(2,1)}, bf16[128,8192]{1,0:T(8,128)(2,1)}, bf16[128,8192]{1,0:T(8,128)(2,1)}) custom-call(bf16[8,16,2,64,128]{4,3,2,1,0:T(8,128)(2,1)} %bitcast.8.in_ref, bf16[128,8192]{1,0:T(8,128)(2,1)} %bitcast.33, bf16[128,8192]{1,0:T(8,128)(2,1)} %bitcast.31, bf16[128,8192]{1,0:T(8,128)(2,1)} %bitcast.29), custom_call_target="tpu_custom_call" | custom-call | bytes 20000000 | tf_op jit(solution)/shard_map/finish/pallas_call | solution.py:312
  (18 shorter events, 0.4 us)
Async XLA Ops:
  91.4 60.3 %all-to-all-start.1 = ((bf16[128,2,64,128]{3,2,1,0:T(8,128)(2,1)}), bf16[128,2,64,128]{3,2,1,0:T(8,128)(2,1)}, u32[]{:S(2)}, u32[]{:S(2)}) async-start(bf16[128,2,64,128]{3,2,1,0:T(8,128)(2,1)} %bitcast.34), calls=%async_computation.1 | async-start | bytes 8388608 | tf_op jit(solution)/shard_map/all_to_all | solution.py:332
  96.7 2.3 %copy-start = (bf16[128,136,128]{2,1,0:T(8,128)(2,1)S(1)}, bf16[128,136,128]{2,1,0:T(8,128)(2,1)}, u32[]{:S(2)}) copy-start(bf16[128,136,128]{2,1,0:T(8,128)(2,1)} %all_to_all.10) | copy-start | bytes 13369348
  128.1 7.9 %collective-permute-start = (f32[1,2,64,128]{3,1,2,0:T(2,128)S(1)}, f32[1,2,64,128]{3,1,2,0:T(2,128)S(1)}, u32[]{:S(2)}, u32[]{:S(2)}) collective-permute-start(f32[1,2,64,128]{3,1,2,0:T(2,128)S(1)} %copy.27), channel_id=1, source_target_pairs={{0,16},{16,32},{32,48},{48,64},{64,80},{80,96},{96,112},{112,0},{1... | collective-permute-start | bytes 196616 | tf_op jit(solution)/shard_map/ppermute | solution.py:342
  129.8 17.1 %collective-permute-start.1 = (f32[1,2,64,128]{3,1,2,0:T(2,128)S(1)}, f32[1,2,64,128]{3,1,2,0:T(2,128)S(1)}, u32[]{:S(2)}, u32[]{:S(2)}) collective-permute-start(f32[1,2,64,128]{3,1,2,0:T(2,128)S(1)} %copy.28), channel_id=1, source_target_pairs={{0,32},{16,48},{32,64},{48,80},{64,96},{80,112},{96,0},{112,16},{1... | collective-permute-start | bytes 196616 | tf_op jit(solution)/shard_map/ppermute | solution.py:342
  131.0 16.3 %collective-permute-start.2 = (f32[1,2,64,128]{3,1,2,0:T(2,128)S(1)}, f32[1,2,64,128]{3,1,2,0:T(2,128)S(1)}, u32[]{:S(2)}, u32[]{:S(2)}) collective-permute-start(f32[1,2,64,128]{3,1,2,0:T(2,128)S(1)} %copy.29), channel_id=1, source_target_pairs={{0,48},{16,64},{32,80},{48,96},{64,112},{80,0},{96,16},{112,32},{1... | collective-permute-start | bytes 196616 | tf_op jit(solution)/shard_map/ppermute | solution.py:342
  132.8 16.7 %collective-permute-start.3 = (f32[1,2,64,128]{3,1,2,0:T(2,128)S(1)}, f32[1,2,64,128]{3,1,2,0:T(2,128)S(1)}, u32[]{:S(2)}, u32[]{:S(2)}) collective-permute-start(f32[1,2,64,128]{3,1,2,0:T(2,128)S(1)} %copy.30), channel_id=1, source_target_pairs={{0,64},{16,80},{32,96},{48,112},{64,0},{80,16},{96,32},{112,48},{1... | collective-permute-start | bytes 196616 | tf_op jit(solution)/shard_map/ppermute | solution.py:342
  133.2 16.7 %collective-permute-start.4 = (f32[1,2,64,128]{3,1,2,0:T(2,128)S(1)}, f32[1,2,64,128]{3,1,2,0:T(2,128)S(1)}, u32[]{:S(2)}, u32[]{:S(2)}) collective-permute-start(f32[1,2,64,128]{3,1,2,0:T(2,128)S(1)} %copy.31), channel_id=1, source_target_pairs={{0,80},{16,96},{32,112},{48,0},{64,16},{80,32},{96,48},{112,64},{1... | collective-permute-start | bytes 196616 | tf_op jit(solution)/shard_map/ppermute | solution.py:342
  136.0 13.9 %collective-permute-start.5 = (f32[1,2,64,128]{3,1,2,0:T(2,128)S(1)}, f32[1,2,64,128]{3,1,2,0:T(2,128)S(1)}, u32[]{:S(2)}, u32[]{:S(2)}) collective-permute-start(f32[1,2,64,128]{3,1,2,0:T(2,128)S(1)} %copy.32), channel_id=1, source_target_pairs={{0,96},{16,112},{32,0},{48,16},{64,32},{80,48},{96,64},{112,80},{1... | collective-permute-start | bytes 196616 | tf_op jit(solution)/shard_map/ppermute | solution.py:342
  146.9 3.7 %collective-permute-start.6 = (f32[1,2,64,128]{3,1,2,0:T(2,128)S(1)}, f32[1,2,64,128]{3,1,2,0:T(2,128)S(1)}, u32[]{:S(2)}, u32[]{:S(2)}) collective-permute-start(f32[1,2,64,128]{3,1,2,0:T(2,128)S(1)} %copy.33), channel_id=1, source_target_pairs={{0,112},{16,0},{32,16},{48,32},{64,48},{80,64},{96,80},{112,96},{1... | collective-permute-start | bytes 196616 | tf_op jit(solution)/shard_map/ppermute | solution.py:342

commit v4 on v3

--- a/solution.py
+++ b/solution.py
@@ -8,6 +8,8 @@
 from jax.sharding import PartitionSpec as P
 
 LANES = 128
+GROUP = 16
+PITCH = 24
 NT = (((1,), (1,)), ((), ()))
 
 
@@ -92,11 +94,11 @@
     )(lax.axis_index("dp").astype(jnp.int32).reshape(1), key, value, grad, query, taps, taps)
 
 
-def rows_of(wide, block, c, seqs, blocks, group):
-    return pl.ds(block * seqs * group + c, seqs, stride=group)
-
-
-def both_body(seqs, blocks, prod_ref, grad_ref, taps_ref, out_ref, prod_wide, grad_wide, taps):
+def rows_of(block, c, seqs):
+    return pl.ds(block * seqs * PITCH + c, seqs, stride=PITCH)
+
+
+def both_body(seqs, blocks, prod_ref, grad_ref, taps_ref, out_ref, prod_wide, grad_wide, taps, made):
     group = prod_ref.shape[2]
     local = LANES // 2
     g = pl.program_id(0)
@@ -119,7 +121,8 @@
 
     for b in range(seqs):
         for j in range(blocks):
-            at = slice((j * seqs + b) * group, (j * seqs + b + 1) * group)
+            start = (j * seqs + b) * PITCH
+            at = slice(start, start + group)
             prod_wide[at, :] = prod_ref[b, j].astype(jnp.float32)
             grad_wide[at, :] = grad_ref[b, j].astype(jnp.float32)
     row, lane = grid_of((LANES, LANES))
@@ -128,7 +131,7 @@
 
     def step(c, carry):
         def load(wide, block):
-            return wide[rows_of(wide, block, c, seqs, blocks, group), :]
+            return wide[rows_of(block, c, seqs), :]
 
         tiles = []
         for i in range(pairs):
@@ -139,6 +142,12 @@
         lines = jnp.concatenate(tiles, axis=0)
         turned_before = jnp.zeros((LANES, LANES), jnp.float32)
         before = jnp.zeros((LANES, LANES), jnp.bfloat16)
+        made_slot = made.at[c % 2]
+        for near in range(blocks):
+            line = taps[pl.ds((g * group + c) * blocks + near, 1), :]
+            turned = pltpu.roll(jnp.broadcast_to(line, (LANES, LANES)), 0, 1, stride=1, stride_axis=0)
+            made_slot[near] = jnp.where(same_block, turned, turned_before).astype(jnp.bfloat16)
+            turned_before = turned
         conv = [None] * pairs
         back = [None] * pairs
 
@@ -146,14 +155,7 @@
             sums[i] = piece if sums[i] is None else sums[i] + piece
 
         for k in range(pairs):
-            here = []
-            for near in (2 * k, 2 * k + 1):
-                line = taps[pl.ds((g * group + c) * blocks + near, 1), :]
-                turned = pltpu.roll(
-                    jnp.broadcast_to(line, (LANES, LANES)), 0, 1, stride=1, stride_axis=0
-                )
-                here.append(jnp.where(same_block, turned, turned_before).astype(jnp.bfloat16))
-                turned_before = turned
+            here = [made_slot[2 * k], made_slot[2 * k + 1]]
             right = jnp.concatenate(
                 [
                     jnp.concatenate(here, axis=1),
@@ -171,7 +173,7 @@
                 add(back, pairs - 1 - i - k, part[at + seqs : at + 2 * seqs])
         for i in range(pairs):
             for side in (0, 1):
-                here = rows_of(prod_wide, 2 * i + side, c, seqs, blocks, group)
+                here = rows_of(2 * i + side, c, seqs)
                 prod_wide[here, :] = conv[i][:, side * LANES : (side + 1) * LANES]
                 grad_wide[here, :] = back[i][:, (1 - side) * LANES : (2 - side) * LANES]
         return carry
@@ -179,16 +181,17 @@
     lax.fori_loop(0, group, step, 0, unroll=True)
     for b in range(seqs):
         for j in range(blocks):
-            at = slice((j * seqs + b) * group, (j * seqs + b + 1) * group)
+            start = (j * seqs + b) * PITCH
+            at = slice(start, start + group)
             out_ref[b, j, 0] = prod_wide[at, :].astype(jnp.bfloat16)
             out_ref[b, j, 1] = grad_wide[at, :].astype(jnp.bfloat16)
 
 
 def both(received, local, share):
     seqs, blocks = received.shape[:2]
-    group = 8
+    group = GROUP
     steps = local // group
-    size = seqs * blocks * group
+    size = (seqs * blocks + 1) * PITCH
     return pl.pallas_call(
         functools.partial(both_body, seqs, blocks),
         grid=(steps,),
@@ -202,7 +205,8 @@
         scratch_shapes=[
             pltpu.VMEM((size, LANES), jnp.float32),
             pltpu.VMEM((size, LANES), jnp.float32),
-            pltpu.VMEM((local * blocks, LANES), jnp.float32),
+            pltpu.VMEM(((local + 1) * blocks, LANES), jnp.float32),
+            pltpu.VMEM((2, blocks, LANES, LANES), jnp.bfloat16),
         ],
         compiler_params=params(60),
         cost_estimate=pl.CostEstimate(
@@ -219,14 +223,15 @@
     same_block = lane >= row
     for b in range(seqs):
         for j in range(blocks):
-            at = slice((j * seqs + b) * group, (j * seqs + b + 1) * group)
+            start = (j * seqs + b) * PITCH
+            at = slice(start, start + group)
             prod_wide[at, :] = prod_ref[b, j].astype(jnp.float32)
             grad_wide[at, :] = grad_ref[b, j].astype(jnp.float32)
     nothing = jnp.zeros((seqs, LANES), jnp.float32)
 
     def step(c, carry):
         def load(wide, block):
-            return wide[rows_of(wide, block, c, seqs, blocks, group), :]
+            return wide[rows_of(block, c, seqs), :]
 
         prod = jnp.concatenate([load(prod_wide, j) for j in range(blocks)], axis=0)
         lines = turn(same, prod.astype(jnp.bfloat16)).astype(jnp.bfloat16)
@@ -254,20 +259,20 @@
                 after = turned
         return carry
 
-    lax.fori_loop(0, group, step, 0, unroll=4)
+    lax.fori_loop(0, group, step, 0, unroll=True)
     rows, cols = grid_of((LANES, LANES))
     flip = jnp.where(rows + cols == LANES - 1, 1.0, 0.0)
     lags = jnp.dot(
         found[...], flip, precision=lax.Precision.HIGHEST, preferred_element_type=jnp.float32
     )
-    out_ref[...] = lags.reshape(blocks, group, LANES)
+    out_ref[...] = lags.astype(jnp.bfloat16).reshape(blocks, group, LANES)
 
 
 def filter_grad(received, local):
     seqs, blocks = received.shape[:2]
-    group = 8
+    group = GROUP
     steps = local // group
-    size = seqs * blocks * group
+    size = (seqs * blocks + 1) * PITCH
     return pl.pallas_call(
         functools.partial(filter_body, seqs, blocks),
         grid=(steps,),
@@ -276,7 +281,7 @@
             pl.BlockSpec((seqs, blocks, group, LANES), lambda g: (0, 0, steps + g, 0)),
         ],
         out_specs=pl.BlockSpec((blocks, group, LANES), lambda g: (0, g, 0)),
-        out_shape=jax.ShapeDtypeStruct((blocks, local, LANES), jnp.float32),
+        out_shape=jax.ShapeDtypeStruct((blocks, local, LANES), jnp.bfloat16),
         scratch_shapes=[pltpu.VMEM((size, LANES), jnp.float32)] * 2
         + [pltpu.VMEM((blocks * group, LANES), jnp.float32)],
         compiler_params=params(16),
@@ -356,6 +361,7 @@
     lags = filter_grad(received, local)
     lags = spread_lags(lags.reshape(seqs, blocks // seqs, local, LANES), seqs)
     grad_filter = lags.transpose(1, 3, 0, 2).reshape(blocks // seqs * LANES, seqs * local)
+    grad_filter = grad_filter.astype(jnp.float32)
     grad_query, grad_key, grad_value = finish(returned, grad, value, key)
     return (grad_query[None], grad_key[None], grad_value[None], grad_filter)
 

time: 159 us -> 155 us (0.975)
  Pallas kernels: 58.1 us -> 50.8 us
  starting transfers between devices: 14.7 us -> 19.9 us
  waiting for transfers between devices: 12.5 us -> 10.1 us
    pallas_call x1, Pallas kernels: 28.7 us -> 22.9 us  [filter_grad(): pl.pallas_call(functools.partial(filter_body, seqs, blocks), grid=(steps,...]
    ppermute x7, starting transfers between devices: 9.66 us -> 14.9 us  [spread_lags(): lax.ppermute(piece, 'dp', [(s, (s + offset) % seqs) for s in range(seqs)])]
    ppermute x7, waiting for transfers between devices: 12.5 us -> 10.1 us  [spread_lags(): lax.ppermute(piece, 'dp', [(s, (s + offset) % seqs) for s in range(seqs)])]
  transfers between devices with their start and end apart: 8 -> 8, of which waited for: 5 -> 5; matrix products, arithmetic and copies ran while one was open for 1% -> 1% of each run, Pallas kernels for 18% -> 15%
where the time goes in v4:
time: 155 us; the launch traced here: 154 us
  blocking collectives  68 us (44%)
  Pallas kernels  50.8 us (33%)
  starting transfers between devices  19.9 us (13%)
  waiting for transfers between devices  10.1 us (7%)
  local copies, waits for them, and re-layouts  4.01 us (3%)
    all_to_all x1, blocking collectives, exchange(): lax.all_to_all(flat, ('dp', 'ctx'), split_axis=0, concat_axis=0, tiled=True)  68 us
    pallas_call x1, Pallas kernels, filter_grad(): pl.pallas_call(functools.partial(filter_body, seqs, blocks), grid=(steps,...  22.9 us
    pallas_call x1, Pallas kernels, both(): pl.pallas_call(functools.partial(both_body, seqs, blocks), grid=(steps,),...  15.5 us
    ppermute x7, starting transfers between devices, spread_lags(): lax.ppermute(piece, 'dp', [(s, (s + offset) % seqs) for s in range(seqs)])  14.9 us
    ppermute x7, waiting for transfers between devices, spread_lags(): lax.ppermute(piece, 'dp', [(s, (s + offset) % seqs) for s in range(seqs)])  10.1 us
    pallas_call x1, Pallas kernels, finish(): pl.pallas_call(functools.partial(finish_body, local), grid=(channels // w...  6.71 us
    pallas_call x1, Pallas kernels, send(): pl.pallas_call(functools.partial(send_body, local, share), grid_spec=pltp...  5.76 us
    all_to_all x1, starting transfers between devices, exchange(): lax.all_to_all(flat, ('dp', 'ctx'), split_axis=0, concat_axis=0, tiled=True)  5.02 us
  transfers between devices with their start and end apart: 8, of which 5 were waited for; matrix products, arithmetic and copies ran while one was open for 1% of the time, Pallas kernels for 15%

profile of v4, /device:TPU:1, one launch (start us, length us, event | category | flops | bytes accessed | tf_op | source)
XLA Modules:
  0.0 154.1 jit_solution(4303119238352896427)
XLA Ops:
  0.6 5.8 %send.1 = bf16[8,16,136,128]{3,2,1,0:T(8,128)(2,1)} custom-call(s32[1]{0:T(128)} %bitcast.me_ref, bf16[128,8192]{1,0:T(8,128)(2,1)} %bitcast.28, bf16[128,8192]{1,0:T(8,128)(2,1)} %bitcast.30, bf16[128,8192]{1,0:T(8,128)(2,1)} %bitcast.32, bf16[128,8192]{1,0:T(8,128)(2,1)} %bitcast.35, f32[128,8192]{1,0:T(8,128)} %high_ref.1, f32[128,8192]{1,0:T(8,128)} %high_ref.1), custom_call_target="tpu_custom_call" | custom-call | bytes 14000000 | tf_op jit(solution)/shard_map/send/pallas_call | solution.py:76
  6.4 68.0 %all_to_all.10 = bf16[128,136,128]{2,1,0:T(8,128)(2,1)} all-to-all(bf16[128,136,128]{2,1,0:T(8,128)(2,1)} %bitcast.27), channel_id=1, replica_groups=mesh['dp'=8,'ctx'=16] {'dp','ctx'}, dimensions={0} | all-to-all | bytes 8912896 | tf_op jit(solution)/shard_map/all_to_all | solution.py:337
  74.4 15.5 %both.1 = bf16[8,16,2,64,128]{4,3,2,1,0:T(8,128)(2,1)} custom-call(bf16[8,16,136,128]{3,2,1,0:T(8,128)(2,1)} %bitcast.21, bf16[8,16,136,128]{3,2,1,0:T(8,128)(2,1)} %bitcast.22, bf16[8,16,136,128]{3,2,1,0:T(8,128)(2,1)} %bitcast.23), custom_call_target="tpu_custom_call" | custom-call | flops 20000000000 | bytes 10000000 | tf_op jit(solution)/shard_map/both/pallas_call | solution.py:195
  89.9 5.0 %all-to-all-start.1 = ((bf16[128,2,64,128]{3,2,1,0:T(8,128)(2,1)}), bf16[128,2,64,128]{3,2,1,0:T(8,128)(2,1)}, u32[]{:S(2)}, u32[]{:S(2)}) async-start(bf16[128,2,64,128]{3,2,1,0:T(8,128)(2,1)} %bitcast.34), calls=%async_computation.1 | async-start | bytes 8388608 | tf_op jit(solution)/shard_map/all_to_all | solution.py:337
  95.2 2.3 %copy-done = bf16[128,136,128]{2,1,0:T(8,128)(2,1)S(1)} copy-done((bf16[128,136,128]{2,1,0:T(8,128)(2,1)S(1)}, bf16[128,136,128]{2,1,0:T(8,128)(2,1)}, u32[]{:S(2)}) %copy-start) | copy-done | bytes 4456472
  97.4 22.9 %filter_grad.1 = bf16[16,64,128]{2,1,0:T(8,128)(2,1)S(1)} custom-call(bf16[8,16,136,128]{3,2,1,0:T(8,128)(2,1)S(1)} %bitcast.24, bf16[8,16,136,128]{3,2,1,0:T(8,128)(2,1)S(1)} %bitcast.25), custom_call_target="tpu_custom_call" | custom-call | flops 24999999488 | bytes 10000000 | tf_op jit(solution)/shard_map/filter_grad/pallas_call | solution.py:276
  120.7 1.7 %collective-permute-start = (bf16[1,2,64,128]{3,1,2,0:T(2,128)(2,1)S(1)}, bf16[1,2,64,128]{3,1,2,0:T(2,128)(2,1)S(1)}, u32[]{:S(2)}, u32[]{:S(2)}) collective-permute-start(bf16[1,2,64,128]{3,1,2,0:T(2,128)(2,1)S(1)} %copy.27), channel_id=1, source_target_pairs={{0,16},{16,32},{32,48},{48,64},{64,80},{80,96},{96,112},{112,0},{1... | collective-permute-start | bytes 98312 | tf_op jit(solution)/shard_map/ppermute | solution.py:347
  122.4 1.3 collective-permute-start.1
  123.6 1.7 %collective-permute-start.2 = (bf16[1,2,64,128]{3,1,2,0:T(2,128)(2,1)S(1)}, bf16[1,2,64,128]{3,1,2,0:T(2,128)(2,1)S(1)}, u32[]{:S(2)}, u32[]{:S(2)}) collective-permute-start(bf16[1,2,64,128]{3,1,2,0:T(2,128)(2,1)S(1)} %copy.29), channel_id=1, source_target_pairs={{0,48},{16,64},{32,80},{48,96},{64,112},{80,0},{96,16},{112,32},{1... | collective-permute-start | bytes 98312 | tf_op jit(solution)/shard_map/ppermute | solution.py:347
  125.3 0.4 collective-permute-start.3
  125.8 2.6 %collective-permute-start.4 = (bf16[1,2,64,128]{3,1,2,0:T(2,128)(2,1)S(1)}, bf16[1,2,64,128]{3,1,2,0:T(2,128)(2,1)S(1)}, u32[]{:S(2)}, u32[]{:S(2)}) collective-permute-start(bf16[1,2,64,128]{3,1,2,0:T(2,128)(2,1)S(1)} %copy.31), channel_id=1, source_target_pairs={{0,80},{16,96},{32,112},{48,0},{64,16},{80,32},{96,48},{112,64},{1... | collective-permute-start | bytes 98312 | tf_op jit(solution)/shard_map/ppermute | solution.py:347
  128.3 0.1 broadcast_in_dim.15
  128.5 0.1 copy_dynamic-update-slice_fusion
  128.5 1.1 collective-permute-done
  129.6 3.9 %collective-permute-start.5 = (bf16[1,2,64,128]{3,1,2,0:T(2,128)(2,1)S(1)}, bf16[1,2,64,128]{3,1,2,0:T(2,128)(2,1)S(1)}, u32[]{:S(2)}, u32[]{:S(2)}) collective-permute-start(bf16[1,2,64,128]{3,1,2,0:T(2,128)(2,1)S(1)} %copy.32), channel_id=1, source_target_pairs={{0,96},{16,112},{32,0},{48,16},{64,32},{80,48},{96,64},{112,80},{1... | collective-permute-start | bytes 98312 | tf_op jit(solution)/shard_map/ppermute | solution.py:347
  133.5 4.1 %collective-permute-done.1 = bf16[1,2,64,128]{3,1,2,0:T(2,128)(2,1)S(1)} collective-permute-done((bf16[1,2,64,128]{3,1,2,0:T(2,128)(2,1)S(1)}, bf16[1,2,64,128]{3,1,2,0:T(2,128)(2,1)S(1)}, u32[]{:S(2)}, u32[]{:S(2)}) %collective-permute-start.1) | collective-permute-done | bytes 32800 | tf_op jit(solution)/shard_map/ppermute | solution.py:347
  137.6 3.3 %collective-permute-start.6 = (bf16[1,2,64,128]{3,1,2,0:T(2,128)(2,1)S(1)}, bf16[1,2,64,128]{3,1,2,0:T(2,128)(2,1)S(1)}, u32[]{:S(2)}, u32[]{:S(2)}) collective-permute-start(bf16[1,2,64,128]{3,1,2,0:T(2,128)(2,1)S(1)} %copy.33), channel_id=1, source_target_pairs={{0,112},{16,0},{32,16},{48,32},{64,48},{80,64},{96,80},{112,96},{1... | collective-permute-start | bytes 98312 | tf_op jit(solution)/shard_map/ppermute | solution.py:347
  141.0 0.4 collective-permute-done.2
  141.4 3.8 %collective-permute-done.3 = bf16[1,2,64,128]{3,1,2,0:T(2,128)(2,1)S(1)} collective-permute-done((bf16[1,2,64,128]{3,1,2,0:T(2,128)(2,1)S(1)}, bf16[1,2,64,128]{3,1,2,0:T(2,128)(2,1)S(1)}, u32[]{:S(2)}, u32[]{:S(2)}) %collective-permute-start.3) | collective-permute-done | bytes 32800 | tf_op jit(solution)/shard_map/ppermute | solution.py:347
  145.2 0.8 collective-permute-done.4
  146.1 0.0 collective-permute-done.6
  146.1 0.2 convert_element_type.13
  146.4 1.0 copy.25
  147.4 6.7 %finish.1 = (bf16[128,8192]{1,0:T(8,128)(2,1)}, bf16[128,8192]{1,0:T(8,128)(2,1)}, bf16[128,8192]{1,0:T(8,128)(2,1)}) custom-call(bf16[8,16,2,64,128]{4,3,2,1,0:T(8,128)(2,1)} %bitcast.8.in_ref, bf16[128,8192]{1,0:T(8,128)(2,1)} %bitcast.33, bf16[128,8192]{1,0:T(8,128)(2,1)} %bitcast.31, bf16[128,8192]{1,0:T(8,128)(2,1)} %bitcast.29), custom_call_target="tpu_custom_call" | custom-call | bytes 20000000 | tf_op jit(solution)/shard_map/finish/pallas_call | solution.py:317
  (19 shorter events, 0.6 us)
Async XLA Ops:
  89.9 57.5 %all-to-all-start.1 = ((bf16[128,2,64,128]{3,2,1,0:T(8,128)(2,1)}), bf16[128,2,64,128]{3,2,1,0:T(8,128)(2,1)}, u32[]{:S(2)}, u32[]{:S(2)}) async-start(bf16[128,2,64,128]{3,2,1,0:T(8,128)(2,1)} %bitcast.34), calls=%async_computation.1 | async-start | bytes 8388608 | tf_op jit(solution)/shard_map/all_to_all | solution.py:337
  95.2 2.3 %copy-start = (bf16[128,136,128]{2,1,0:T(8,128)(2,1)S(1)}, bf16[128,136,128]{2,1,0:T(8,128)(2,1)}, u32[]{:S(2)}) copy-start(bf16[128,136,128]{2,1,0:T(8,128)(2,1)} %all_to_all.10) | copy-start | bytes 13369348
  120.7 8.9 %collective-permute-start = (bf16[1,2,64,128]{3,1,2,0:T(2,128)(2,1)S(1)}, bf16[1,2,64,128]{3,1,2,0:T(2,128)(2,1)S(1)}, u32[]{:S(2)}, u32[]{:S(2)}) collective-permute-start(bf16[1,2,64,128]{3,1,2,0:T(2,128)(2,1)S(1)} %copy.27), channel_id=1, source_target_pairs={{0,16},{16,32},{32,48},{48,64},{64,80},{80,96},{96,112},{112,0},{1... | collective-permute-start | bytes 98312 | tf_op jit(solution)/shard_map/ppermute | solution.py:347
  122.4 15.2 %collective-permute-start.1 = (bf16[1,2,64,128]{3,1,2,0:T(2,128)(2,1)S(1)}, bf16[1,2,64,128]{3,1,2,0:T(2,128)(2,1)S(1)}, u32[]{:S(2)}, u32[]{:S(2)}) collective-permute-start(bf16[1,2,64,128]{3,1,2,0:T(2,128)(2,1)S(1)} %copy.28), channel_id=1, source_target_pairs={{0,32},{16,48},{32,64},{48,80},{64,96},{80,112},{96,0},{112,16},{1... | collective-permute-start | bytes 98312 | tf_op jit(solution)/shard_map/ppermute | solution.py:347
  123.6 17.8 %collective-permute-start.2 = (bf16[1,2,64,128]{3,1,2,0:T(2,128)(2,1)S(1)}, bf16[1,2,64,128]{3,1,2,0:T(2,128)(2,1)S(1)}, u32[]{:S(2)}, u32[]{:S(2)}) collective-permute-start(bf16[1,2,64,128]{3,1,2,0:T(2,128)(2,1)S(1)} %copy.29), channel_id=1, source_target_pairs={{0,48},{16,64},{32,80},{48,96},{64,112},{80,0},{96,16},{112,32},{1... | collective-permute-start | bytes 98312 | tf_op jit(solution)/shard_map/ppermute | solution.py:347
  125.3 19.8 %collective-permute-start.3 = (bf16[1,2,64,128]{3,1,2,0:T(2,128)(2,1)S(1)}, bf16[1,2,64,128]{3,1,2,0:T(2,128)(2,1)S(1)}, u32[]{:S(2)}, u32[]{:S(2)}) collective-permute-start(bf16[1,2,64,128]{3,1,2,0:T(2,128)(2,1)S(1)} %copy.30), channel_id=1, source_target_pairs={{0,64},{16,80},{32,96},{48,112},{64,0},{80,16},{96,32},{112,48},{1... | collective-permute-start | bytes 98312 | tf_op jit(solution)/shard_map/ppermute | solution.py:347
  125.8 20.2 %collective-permute-start.4 = (bf16[1,2,64,128]{3,1,2,0:T(2,128)(2,1)S(1)}, bf16[1,2,64,128]{3,1,2,0:T(2,128)(2,1)S(1)}, u32[]{:S(2)}, u32[]{:S(2)}) collective-permute-start(bf16[1,2,64,128]{3,1,2,0:T(2,128)(2,1)S(1)} %copy.31), channel_id=1, source_target_pairs={{0,80},{16,96},{32,112},{48,0},{64,16},{80,32},{96,48},{112,64},{1... | collective-permute-start | bytes 98312 | tf_op jit(solution)/shard_map/ppermute | solution.py:347
  129.6 16.4 %collective-permute-start.5 = (bf16[1,2,64,128]{3,1,2,0:T(2,128)(2,1)S(1)}, bf16[1,2,64,128]{3,1,2,0:T(2,128)(2,1)S(1)}, u32[]{:S(2)}, u32[]{:S(2)}) collective-permute-start(bf16[1,2,64,128]{3,1,2,0:T(2,128)(2,1)S(1)} %copy.32), channel_id=1, source_target_pairs={{0,96},{16,112},{32,0},{48,16},{64,32},{80,48},{96,64},{112,80},{1... | collective-permute-start | bytes 98312 | tf_op jit(solution)/shard_map/ppermute | solution.py:347
  137.6 8.5 %collective-permute-start.6 = (bf16[1,2,64,128]{3,1,2,0:T(2,128)(2,1)S(1)}, bf16[1,2,64,128]{3,1,2,0:T(2,128)(2,1)S(1)}, u32[]{:S(2)}, u32[]{:S(2)}) collective-permute-start(bf16[1,2,64,128]{3,1,2,0:T(2,128)(2,1)S(1)} %copy.33), channel_id=1, source_target_pairs={{0,112},{16,0},{32,16},{48,32},{64,48},{80,64},{96,80},{112,96},{1... | collective-permute-start | bytes 98312 | tf_op jit(solution)/shard_map/ppermute | solution.py:347

commit v5 on v4

--- a/solution.py
+++ b/solution.py
@@ -339,14 +339,23 @@
 
 
 def spread_lags(lags, seqs):
-    me = lax.axis_index("dp")
-    held = jnp.zeros_like(lags)
-    for offset in range(seqs):
-        piece = lax.dynamic_index_in_dim(lags, (me + offset) % seqs, 0, keepdims=True)
+    pair, side = lax.axis_index("dp") // 2, lax.axis_index("dp") % 2
+    pairs = seqs // 2
+    lags = lags.reshape(pairs, 2, *lags.shape[1:])
+    mine = lax.dynamic_slice_in_dim(lags, side, 1, 1)
+    theirs = lax.dynamic_slice_in_dim(lags, 1 - side, 1, 1)
+    theirs = lax.ppermute(theirs, "dp", [(d, d + 1 - 2 * (d % 2)) for d in range(seqs)])
+    first = side == 0
+    joined = jnp.concatenate(
+        [jnp.where(first, mine, theirs), jnp.where(first, theirs, mine)], axis=1
+    )
+    held = jnp.zeros_like(joined)
+    for offset in range(pairs):
+        piece = lax.dynamic_slice_in_dim(joined, (pair + offset) % pairs, 1, 0)
         if offset:
-            piece = lax.ppermute(piece, "dp", [(s, (s + offset) % seqs) for s in range(seqs)])
-        held = lax.dynamic_update_slice_in_dim(held, piece, (me - offset) % seqs, 0)
-    return held
+            piece = lax.ppermute(piece, "dp", [(d, (d + 2 * offset) % seqs) for d in range(seqs)])
+        held = lax.dynamic_update_slice_in_dim(held, piece, (pair - offset) % pairs, 0)
+    return held.reshape(seqs, *held.shape[2:])
 
 
 def on_device(seqs, blocks, query_act, key_act, value_act, grad_out, filter_taps):

time: 155 us -> 154 us (level)
  starting transfers between devices: 19.9 us -> 10 us
  waiting for transfers between devices: 10.1 us -> 19.7 us
    ppermute x7 -> x4, starting transfers between devices: 14.9 us -> 4.99 us  [the longest x3 3.63 us: spread_lags(): lax.ppermute(piece, 'dp', [(d, (d + 2 * offset) % seqs) for d in range(se...]
    ppermute x7 -> x4, waiting for transfers between devices: 10.1 us -> 19.7 us  [the longest x3 18.7 us: spread_lags(): lax.ppermute(piece, 'dp', [(d, (d + 2 * offset) % seqs) for d in range(se...]
    unnamed x11 -> x4, local copies, waits for them, and re-layouts: 3.54 us -> 3.29 us
  transfers between devices with their start and end apart: 8 -> 5, of which waited for: 5 -> 3; matrix products, arithmetic and copies ran while one was open for 1% -> 1% of each run, Pallas kernels for 15% -> 15%
where the time goes in v5:
time: 154 us; the launch traced here: 153 us
  blocking collectives  68 us (44%)
  Pallas kernels  50.8 us (33%)
  waiting for transfers between devices  19.7 us (13%)
  starting transfers between devices  10 us (6%)
  local copies, waits for them, and re-layouts  3.77 us (2%)
    all_to_all x1, blocking collectives, exchange(): lax.all_to_all(flat, ('dp', 'ctx'), split_axis=0, concat_axis=0, tiled=True)  68 us
    pallas_call x1, Pallas kernels, filter_grad(): pl.pallas_call(functools.partial(filter_body, seqs, blocks), grid=(steps,...  22.9 us
    ppermute x3, waiting for transfers between devices, spread_lags(): lax.ppermute(piece, 'dp', [(d, (d + 2 * offset) % seqs) for d in range(se...  18.7 us
    pallas_call x1, Pallas kernels, both(): pl.pallas_call(functools.partial(both_body, seqs, blocks), grid=(steps,),...  15.5 us
    pallas_call x1, Pallas kernels, finish(): pl.pallas_call(functools.partial(finish_body, local), grid=(channels // w...  6.71 us
    pallas_call x1, Pallas kernels, send(): pl.pallas_call(functools.partial(send_body, local, share), grid_spec=pltp...  5.74 us
    all_to_all x1, starting transfers between devices, exchange(): lax.all_to_all(flat, ('dp', 'ctx'), split_axis=0, concat_axis=0, tiled=True)  5.02 us
    ppermute x3, starting transfers between devices, spread_lags(): lax.ppermute(piece, 'dp', [(d, (d + 2 * offset) % seqs) for d in range(se...  3.63 us
  transfers between devices with their start and end apart: 5, of which 3 were waited for; matrix products, arithmetic and copies ran while one was open for 1% of the time, Pallas kernels for 15%

profile of v5, /device:TPU:1, one launch (start us, length us, event | category | flops | bytes accessed | tf_op | source)
XLA Modules:
  0.0 153.3 jit_solution(16701976011878473638)
XLA Ops:
  0.6 5.7 %send.1 = bf16[8,16,136,128]{3,2,1,0:T(8,128)(2,1)} custom-call(s32[1]{0:T(128)} %bitcast.me_ref, bf16[128,8192]{1,0:T(8,128)(2,1)} %bitcast.32, bf16[128,8192]{1,0:T(8,128)(2,1)} %bitcast.34, bf16[128,8192]{1,0:T(8,128)(2,1)} %bitcast.36, bf16[128,8192]{1,0:T(8,128)(2,1)} %bitcast.39, f32[128,8192]{1,0:T(8,128)} %high_ref.1, f32[128,8192]{1,0:T(8,128)} %high_ref.1), custom_call_target="tpu_custom_call" | custom-call | bytes 14000000 | tf_op jit(solution)/shard_map/send/pallas_call | solution.py:76
  6.4 68.0 %all_to_all.10 = bf16[128,136,128]{2,1,0:T(8,128)(2,1)} all-to-all(bf16[128,136,128]{2,1,0:T(8,128)(2,1)} %bitcast.31), channel_id=1, replica_groups=mesh['dp'=8,'ctx'=16] {'dp','ctx'}, dimensions={0} | all-to-all | bytes 8912896 | tf_op jit(solution)/shard_map/all_to_all | solution.py:337
  74.4 15.5 %both.1 = bf16[8,16,2,64,128]{4,3,2,1,0:T(8,128)(2,1)} custom-call(bf16[8,16,136,128]{3,2,1,0:T(8,128)(2,1)} %bitcast.24, bf16[8,16,136,128]{3,2,1,0:T(8,128)(2,1)} %bitcast.25, bf16[8,16,136,128]{3,2,1,0:T(8,128)(2,1)} %bitcast.26), custom_call_target="tpu_custom_call" | custom-call | flops 20000000000 | bytes 10000000 | tf_op jit(solution)/shard_map/both/pallas_call | solution.py:195
  89.9 5.0 %all-to-all-start.1 = ((bf16[128,2,64,128]{3,2,1,0:T(8,128)(2,1)}), bf16[128,2,64,128]{3,2,1,0:T(8,128)(2,1)}, u32[]{:S(2)}, u32[]{:S(2)}) async-start(bf16[128,2,64,128]{3,2,1,0:T(8,128)(2,1)} %bitcast.38), calls=%async_computation.1 | async-start | bytes 8388608 | tf_op jit(solution)/shard_map/all_to_all | solution.py:337
  94.9 0.0 copy-start
  94.9 2.3 %copy-done = bf16[128,136,128]{2,1,0:T(8,128)(2,1)S(1)} copy-done((bf16[128,136,128]{2,1,0:T(8,128)(2,1)S(1)}, bf16[128,136,128]{2,1,0:T(8,128)(2,1)}, u32[]{:S(2)}) %copy-start) | copy-done | bytes 4456472
  97.2 22.9 %filter_grad.1 = bf16[16,64,128]{2,1,0:T(8,128)(2,1)S(1)} custom-call(bf16[8,16,136,128]{3,2,1,0:T(8,128)(2,1)S(1)} %bitcast.27, bf16[8,16,136,128]{3,2,1,0:T(8,128)(2,1)S(1)} %bitcast.28), custom_call_target="tpu_custom_call" | custom-call | flops 24999999488 | bytes 10000000 | tf_op jit(solution)/shard_map/filter_grad/pallas_call | solution.py:276
  120.1 1.4 collective-permute-start
  121.4 1.0 collective-permute-done
  122.5 1.9 %collective-permute-start.3 = (bf16[1,2,2,64,128]{4,3,2,1,0:T(8,128)(2,1)S(1)}, bf16[1,2,2,64,128]{4,3,2,1,0:T(8,128)(2,1)S(1)}, u32[]{:S(2)}, u32[]{:S(2)}) collective-permute-start(bf16[1,2,2,64,128]{4,3,2,1,0:T(8,128)(2,1)S(1)} %get-tuple-element.18), channel_id=1, source_target_pairs={{0,96},{16,112},{32,0},{48,16},{64,32},{80,48},{96,64},{112,80},{1... | collective-permute-start | bytes 196616 | tf_op jit(solution)/shard_map/ppermute | solution.py:356
  124.4 0.0 collective-permute-start.1
  124.4 1.7 %collective-permute-start.2 = (bf16[1,2,2,64,128]{4,3,2,1,0:T(8,128)(2,1)S(1)}, bf16[1,2,2,64,128]{4,3,2,1,0:T(8,128)(2,1)S(1)}, u32[]{:S(2)}, u32[]{:S(2)}) collective-permute-start(bf16[1,2,2,64,128]{4,3,2,1,0:T(8,128)(2,1)S(1)} %get-tuple-element.21), channel_id=1, source_target_pairs={{0,64},{16,80},{32,96},{48,112},{64,0},{80,16},{96,32},{112,48},{1... | collective-permute-start | bytes 196616 | tf_op jit(solution)/shard_map/ppermute | solution.py:356
  126.1 0.1 broadcast_in_dim.15
  126.3 0.1 copy_dynamic-update-slice_fusion.3
  126.4 11.2 %collective-permute-done.1 = bf16[1,2,2,64,128]{4,3,2,1,0:T(8,128)(2,1)S(1)} collective-permute-done((bf16[1,2,2,64,128]{4,3,2,1,0:T(8,128)(2,1)S(1)}, bf16[1,2,2,64,128]{4,3,2,1,0:T(8,128)(2,1)S(1)}, u32[]{:S(2)}, u32[]{:S(2)}) %collective-permute-start.1) | collective-permute-done | bytes 65568 | tf_op jit(solution)/shard_map/ppermute | solution.py:356
  137.6 0.1 copy_dynamic-update-slice_fusion.2
  137.7 7.5 %collective-permute-done.2 = bf16[1,2,2,64,128]{4,3,2,1,0:T(8,128)(2,1)S(1)} collective-permute-done((bf16[1,2,2,64,128]{4,3,2,1,0:T(8,128)(2,1)S(1)}, bf16[1,2,2,64,128]{4,3,2,1,0:T(8,128)(2,1)S(1)}, u32[]{:S(2)}, u32[]{:S(2)}) %collective-permute-start.2) | collective-permute-done | bytes 65568 | tf_op jit(solution)/shard_map/ppermute | solution.py:356
  145.2 0.1 copy_dynamic-update-slice_fusion.1
  145.2 0.0 collective-permute-done.3
  145.2 0.1 copy_dynamic-update-slice_fusion
  145.3 0.2 bitcast_convert_fusion
  145.6 1.0 copy.15
  146.6 0.0 all-to-all-done.1
  146.6 6.7 %finish.1 = (bf16[128,8192]{1,0:T(8,128)(2,1)}, bf16[128,8192]{1,0:T(8,128)(2,1)}, bf16[128,8192]{1,0:T(8,128)(2,1)}) custom-call(bf16[8,16,2,64,128]{4,3,2,1,0:T(8,128)(2,1)} %bitcast.8.in_ref, bf16[128,8192]{1,0:T(8,128)(2,1)} %bitcast.37, bf16[128,8192]{1,0:T(8,128)(2,1)} %bitcast.35, bf16[128,8192]{1,0:T(8,128)(2,1)} %bitcast.33), custom_call_target="tpu_custom_call" | custom-call | bytes 20000000 | tf_op jit(solution)/shard_map/finish/pallas_call | solution.py:317
  (4 shorter events, 0.1 us)
Async XLA Ops:
  89.9 56.7 %all-to-all-start.1 = ((bf16[128,2,64,128]{3,2,1,0:T(8,128)(2,1)}), bf16[128,2,64,128]{3,2,1,0:T(8,128)(2,1)}, u32[]{:S(2)}, u32[]{:S(2)}) async-start(bf16[128,2,64,128]{3,2,1,0:T(8,128)(2,1)} %bitcast.38), calls=%async_computation.1 | async-start | bytes 8388608 | tf_op jit(solution)/shard_map/all_to_all | solution.py:337
  94.9 2.3 %copy-start = (bf16[128,136,128]{2,1,0:T(8,128)(2,1)S(1)}, bf16[128,136,128]{2,1,0:T(8,128)(2,1)}, u32[]{:S(2)}) copy-start(bf16[128,136,128]{2,1,0:T(8,128)(2,1)} %all_to_all.10) | copy-start | bytes 13369348
  120.1 2.3 %collective-permute-start = (bf16[4,1,2,64,128]{4,3,2,1,0:T(8,128)(2,1)S(1)}, bf16[4,1,2,64,128]{4,3,2,1,0:T(8,128)(2,1)S(1)}, u32[]{:S(2)}, u32[]{:S(2)}) collective-permute-start(bf16[4,1,2,64,128]{4,3,2,1,0:T(8,128)(2,1)S(1)} %constant_dynamic-slice_fusion), channel_id=1, source_target_pairs={{0,16},{16,0},{32,48},{48,32},{64,80},{80,64},{96,112},{112,96},{1... | collective-permute-start | bytes 393224 | tf_op jit(solution)/shard_map/ppermute | solution.py:347
  122.5 22.7 %collective-permute-start.3 = (bf16[1,2,2,64,128]{4,3,2,1,0:T(8,128)(2,1)S(1)}, bf16[1,2,2,64,128]{4,3,2,1,0:T(8,128)(2,1)S(1)}, u32[]{:S(2)}, u32[]{:S(2)}) collective-permute-start(bf16[1,2,2,64,128]{4,3,2,1,0:T(8,128)(2,1)S(1)} %get-tuple-element.18), channel_id=1, source_target_pairs={{0,96},{16,112},{32,0},{48,16},{64,32},{80,48},{96,64},{112,80},{1... | collective-permute-start | bytes 196616 | tf_op jit(solution)/shard_map/ppermute | solution.py:356
  124.4 13.2 %collective-permute-start.1 = (bf16[1,2,2,64,128]{4,3,2,1,0:T(8,128)(2,1)S(1)}, bf16[1,2,2,64,128]{4,3,2,1,0:T(8,128)(2,1)S(1)}, u32[]{:S(2)}, u32[]{:S(2)}) collective-permute-start(bf16[1,2,2,64,128]{4,3,2,1,0:T(8,128)(2,1)S(1)} %get-tuple-element.20), channel_id=1, source_target_pairs={{0,32},{16,48},{32,64},{48,80},{64,96},{80,112},{96,0},{112,16},{1... | collective-permute-start | bytes 196616 | tf_op jit(solution)/shard_map/ppermute | solution.py:356
  124.4 20.7 %collective-permute-start.2 = (bf16[1,2,2,64,128]{4,3,2,1,0:T(8,128)(2,1)S(1)}, bf16[1,2,2,64,128]{4,3,2,1,0:T(8,128)(2,1)S(1)}, u32[]{:S(2)}, u32[]{:S(2)}) collective-permute-start(bf16[1,2,2,64,128]{4,3,2,1,0:T(8,128)(2,1)S(1)} %get-tuple-element.21), channel_id=1, source_target_pairs={{0,64},{16,80},{32,96},{48,112},{64,0},{80,16},{96,32},{112,48},{1... | collective-permute-start | bytes 196616 | tf_op jit(solution)/shard_map/ppermute | solution.py:356

commit v6 on v5

--- a/solution.py
+++ b/solution.py
@@ -349,13 +349,21 @@
     joined = jnp.concatenate(
         [jnp.where(first, mine, theirs), jnp.where(first, theirs, mine)], axis=1
     )
-    held = jnp.zeros_like(joined)
+    came = []
     for offset in range(pairs):
         piece = lax.dynamic_slice_in_dim(joined, (pair + offset) % pairs, 1, 0)
         if offset:
             piece = lax.ppermute(piece, "dp", [(d, (d + 2 * offset) % seqs) for d in range(seqs)])
+        came.append(piece)
+    return came
+
+
+def gather_lags(came):
+    pair, pairs = lax.axis_index("dp") // 2, len(came)
+    held = jnp.zeros((pairs, *came[0].shape[1:]), came[0].dtype)
+    for offset, piece in enumerate(came):
         held = lax.dynamic_update_slice_in_dim(held, piece, (pair - offset) % pairs, 0)
-    return held.reshape(seqs, *held.shape[2:])
+    return held.reshape(2 * pairs, *held.shape[2:])
 
 
 def on_device(seqs, blocks, query_act, key_act, value_act, grad_out, filter_taps):
@@ -368,10 +376,12 @@
     returned = exchange(sums)
     received, sums = lax.optimization_barrier((received, sums))
     lags = filter_grad(received, local)
-    lags = spread_lags(lags.reshape(seqs, blocks // seqs, local, LANES), seqs)
+    came = spread_lags(lags.reshape(seqs, blocks // seqs, local, LANES), seqs)
+    grad_query, grad_key, grad_value = finish(returned, grad, value, key)
+    came, grad_query = lax.optimization_barrier((came, grad_query))
+    lags = gather_lags(came)
     grad_filter = lags.transpose(1, 3, 0, 2).reshape(blocks // seqs * LANES, seqs * local)
     grad_filter = grad_filter.astype(jnp.float32)
-    grad_query, grad_key, grad_value = finish(returned, grad, value, key)
     return (grad_query[None], grad_key[None], grad_value[None], grad_filter)
 
 

time: 154 us -> 155 us (level)
    all_to_all x1, waiting for transfers between devices: 0.01 us -> 19.6 us  [exchange(): lax.all_to_all(flat, ('dp', 'ctx'), split_axis=0, concat_axis=0, tiled=True)]
    ppermute x3, waiting for transfers between devices: 18.7 us -> 0.01 us  [spread_lags(): lax.ppermute(piece, 'dp', [(d, (d + 2 * offset) % seqs) for d in range(se...]
  transfers between devices with their start and end apart: 5 -> 5, of which waited for: 3 -> 2; matrix products, arithmetic and copies ran while one was open for 1% -> 0% of each run, Pallas kernels for 15% -> 19%
where the time goes in v6:
time: 155 us
  blocking collectives  68 us (44%)
  Pallas kernels  50.8 us (33%)
  waiting for transfers between devices  20.6 us (13%)
  starting transfers between devices  10.6 us (7%)
  local copies, waits for them, and re-layouts  3.78 us (2%)
    all_to_all x1, blocking collectives, exchange(): lax.all_to_all(flat, ('dp', 'ctx'), split_axis=0, concat_axis=0, tiled=True)  68 us
    pallas_call x1, Pallas kernels, filter_grad(): pl.pallas_call(functools.partial(filter_body, seqs, blocks), grid=(steps,...  22.9 us
    all_to_all x1, waiting for transfers between devices, exchange(): lax.all_to_all(flat, ('dp', 'ctx'), split_axis=0, concat_axis=0, tiled=True)  19.6 us
    pallas_call x1, Pallas kernels, both(): pl.pallas_call(functools.partial(both_body, seqs, blocks), grid=(steps,),...  15.5 us
    pallas_call x1, Pallas kernels, finish(): pl.pallas_call(functools.partial(finish_body, local), grid=(channels // w...  6.7 us
    pallas_call x1, Pallas kernels, send(): pl.pallas_call(functools.partial(send_body, local, share), grid_spec=pltp...  5.74 us
    all_to_all x1, starting transfers between devices, exchange(): lax.all_to_all(flat, ('dp', 'ctx'), split_axis=0, concat_axis=0, tiled=True)  5.02 us
    ppermute x3, starting transfers between devices, spread_lags(): lax.ppermute(piece, 'dp', [(d, (d + 2 * offset) % seqs) for d in range(se...  4.23 us
  transfers between devices with their start and end apart: 5, of which 2 were waited for; matrix products, arithmetic and copies ran while one was open for 0% of the time, Pallas kernels for 19%

profile of v6, /device:TPU:1, one launch (start us, length us, event | category | flops | bytes accessed | tf_op | source)
XLA Modules:
  0.0 154.8 jit_solution(11627826005379446855)
XLA Ops:
  0.6 5.7 %send.1 = bf16[8,16,136,128]{3,2,1,0:T(8,128)(2,1)} custom-call(s32[1]{0:T(128)} %bitcast.me_ref, bf16[128,8192]{1,0:T(8,128)(2,1)} %bitcast.32, bf16[128,8192]{1,0:T(8,128)(2,1)} %bitcast.34, bf16[128,8192]{1,0:T(8,128)(2,1)} %bitcast.36, bf16[128,8192]{1,0:T(8,128)(2,1)} %bitcast.39, f32[128,8192]{1,0:T(8,128)} %high_ref.1, f32[128,8192]{1,0:T(8,128)} %high_ref.1), custom_call_target="tpu_custom_call" | custom-call | bytes 14000000 | tf_op jit(solution)/shard_map/send/pallas_call | solution.py:76
  6.4 68.0 %all_to_all.10 = bf16[128,136,128]{2,1,0:T(8,128)(2,1)} all-to-all(bf16[128,136,128]{2,1,0:T(8,128)(2,1)} %bitcast.31), channel_id=1, replica_groups=mesh['dp'=8,'ctx'=16] {'dp','ctx'}, dimensions={0} | all-to-all | bytes 8912896 | tf_op jit(solution)/shard_map/all_to_all | solution.py:337
  74.4 15.5 %both.1 = bf16[8,16,2,64,128]{4,3,2,1,0:T(8,128)(2,1)} custom-call(bf16[8,16,136,128]{3,2,1,0:T(8,128)(2,1)} %bitcast.24, bf16[8,16,136,128]{3,2,1,0:T(8,128)(2,1)} %bitcast.25, bf16[8,16,136,128]{3,2,1,0:T(8,128)(2,1)} %bitcast.26), custom_call_target="tpu_custom_call" | custom-call | flops 20000000000 | bytes 10000000 | tf_op jit(solution)/shard_map/both/pallas_call | solution.py:195
  89.9 5.0 %all-to-all-start.1 = ((bf16[128,2,64,128]{3,2,1,0:T(8,128)(2,1)}), bf16[128,2,64,128]{3,2,1,0:T(8,128)(2,1)}, u32[]{:S(2)}, u32[]{:S(2)}) async-start(bf16[128,2,64,128]{3,2,1,0:T(8,128)(2,1)} %bitcast.38), calls=%async_computation.1 | async-start | bytes 8388608 | tf_op jit(solution)/shard_map/all_to_all | solution.py:337
  94.9 0.0 copy-start
  94.9 2.3 %copy-done = bf16[128,136,128]{2,1,0:T(8,128)(2,1)S(1)} copy-done((bf16[128,136,128]{2,1,0:T(8,128)(2,1)S(1)}, bf16[128,136,128]{2,1,0:T(8,128)(2,1)}, u32[]{:S(2)}) %copy-start) | copy-done | bytes 4456472
  97.2 22.9 %filter_grad.1 = bf16[16,64,128]{2,1,0:T(8,128)(2,1)S(1)} custom-call(bf16[8,16,136,128]{3,2,1,0:T(8,128)(2,1)S(1)} %bitcast.27, bf16[8,16,136,128]{3,2,1,0:T(8,128)(2,1)S(1)} %bitcast.28), custom_call_target="tpu_custom_call" | custom-call | flops 24999999488 | bytes 10000000 | tf_op jit(solution)/shard_map/filter_grad/pallas_call | solution.py:276
  120.1 1.4 collective-permute-start
  121.4 1.0 collective-permute-done
  122.5 0.6 collective-permute-start.1
  123.1 2.5 %collective-permute-start.2 = (bf16[1,2,2,64,128]{4,3,2,1,0:T(8,128)(2,1)S(1)}, bf16[1,2,2,64,128]{4,3,2,1,0:T(8,128)(2,1)S(1)}, u32[]{:S(2)}, u32[]{:S(2)}) collective-permute-start(bf16[1,2,2,64,128]{4,3,2,1,0:T(8,128)(2,1)S(1)} %get-tuple-element.31), channel_id=1, source_target_pairs={{0,64},{16,80},{32,96},{48,112},{64,0},{80,16},{96,32},{112,48},{1... | collective-permute-start | bytes 196616 | tf_op jit(solution)/shard_map/ppermute | solution.py:356
  125.6 1.1 collective-permute-start.3
  126.7 19.6 %all-to-all-done.1 = bf16[128,2,64,128]{3,2,1,0:T(8,128)(2,1)} async-done(((bf16[128,2,64,128]{3,2,1,0:T(8,128)(2,1)}), bf16[128,2,64,128]{3,2,1,0:T(8,128)(2,1)}, u32[]{:S(2)}, u32[]{:S(2)}) %all-to-all-start.1) | async-done | bytes 4194336 | tf_op jit(solution)/shard_map/all_to_all | solution.py:337
  146.3 6.7 %finish.1 = (bf16[128,8192]{1,0:T(8,128)(2,1)}, bf16[128,8192]{1,0:T(8,128)(2,1)}, bf16[128,8192]{1,0:T(8,128)(2,1)}) custom-call(bf16[8,16,2,64,128]{4,3,2,1,0:T(8,128)(2,1)} %bitcast.9.in_ref, bf16[128,8192]{1,0:T(8,128)(2,1)} %bitcast.37, bf16[128,8192]{1,0:T(8,128)(2,1)} %bitcast.35, bf16[128,8192]{1,0:T(8,128)(2,1)} %bitcast.33), custom_call_target="tpu_custom_call" | custom-call | bytes 20000000 | tf_op jit(solution)/shard_map/finish/pallas_call | solution.py:317
  153.0 0.0 collective-permute-done.1
  153.0 0.0 collective-permute-done.2
  153.0 0.0 collective-permute-done.3
  153.1 0.1 broadcast_in_dim.15
  153.2 0.1 copy_dynamic-update-slice_fusion.3
  153.3 0.1 copy_dynamic-update-slice_fusion.2
  153.4 0.1 copy_dynamic-update-slice_fusion.1
  153.5 0.1 copy_dynamic-update-slice_fusion
  153.5 0.2 bitcast_convert_fusion
  153.8 1.0 copy.15
  (4 shorter events, 0.1 us)
Async XLA Ops:
  89.9 56.5 %all-to-all-start.1 = ((bf16[128,2,64,128]{3,2,1,0:T(8,128)(2,1)}), bf16[128,2,64,128]{3,2,1,0:T(8,128)(2,1)}, u32[]{:S(2)}, u32[]{:S(2)}) async-start(bf16[128,2,64,128]{3,2,1,0:T(8,128)(2,1)} %bitcast.38), calls=%async_computation.1 | async-start | bytes 8388608 | tf_op jit(solution)/shard_map/all_to_all | solution.py:337
  94.9 2.3 %copy-start = (bf16[128,136,128]{2,1,0:T(8,128)(2,1)S(1)}, bf16[128,136,128]{2,1,0:T(8,128)(2,1)}, u32[]{:S(2)}) copy-start(bf16[128,136,128]{2,1,0:T(8,128)(2,1)} %all_to_all.10) | copy-start | bytes 13369348
  120.1 2.3 %collective-permute-start = (bf16[4,1,2,64,128]{4,3,2,1,0:T(8,128)(2,1)S(1)}, bf16[4,1,2,64,128]{4,3,2,1,0:T(8,128)(2,1)S(1)}, u32[]{:S(2)}, u32[]{:S(2)}) collective-permute-start(bf16[4,1,2,64,128]{4,3,2,1,0:T(8,128)(2,1)S(1)} %constant_dynamic-slice_fusion), channel_id=1, source_target_pairs={{0,16},{16,0},{32,48},{48,32},{64,80},{80,64},{96,112},{112,96},{1... | collective-permute-start | bytes 393224 | tf_op jit(solution)/shard_map/ppermute | solution.py:347
  122.5 30.5 %collective-permute-start.1 = (bf16[1,2,2,64,128]{4,3,2,1,0:T(8,128)(2,1)S(1)}, bf16[1,2,2,64,128]{4,3,2,1,0:T(8,128)(2,1)S(1)}, u32[]{:S(2)}, u32[]{:S(2)}) collective-permute-start(bf16[1,2,2,64,128]{4,3,2,1,0:T(8,128)(2,1)S(1)} %get-tuple-element.30), channel_id=1, source_target_pairs={{0,32},{16,48},{32,64},{48,80},{64,96},{80,112},{96,0},{112,16},{1... | collective-permute-start | bytes 196616 | tf_op jit(solution)/shard_map/ppermute | solution.py:356
  123.1 30.0 %collective-permute-start.2 = (bf16[1,2,2,64,128]{4,3,2,1,0:T(8,128)(2,1)S(1)}, bf16[1,2,2,64,128]{4,3,2,1,0:T(8,128)(2,1)S(1)}, u32[]{:S(2)}, u32[]{:S(2)}) collective-permute-start(bf16[1,2,2,64,128]{4,3,2,1,0:T(8,128)(2,1)S(1)} %get-tuple-element.31), channel_id=1, source_target_pairs={{0,64},{16,80},{32,96},{48,112},{64,0},{80,16},{96,32},{112,48},{1... | collective-permute-start | bytes 196616 | tf_op jit(solution)/shard_map/ppermute | solution.py:356
  125.6 27.4 %collective-permute-start.3 = (bf16[1,2,2,64,128]{4,3,2,1,0:T(8,128)(2,1)S(1)}, bf16[1,2,2,64,128]{4,3,2,1,0:T(8,128)(2,1)S(1)}, u32[]{:S(2)}, u32[]{:S(2)}) collective-permute-start(bf16[1,2,2,64,128]{4,3,2,1,0:T(8,128)(2,1)S(1)} %get-tuple-element.28), channel_id=1, source_target_pairs={{0,96},{16,112},{32,0},{48,16},{64,32},{80,48},{96,64},{112,80},{1... | collective-permute-start | bytes 196616 | tf_op jit(solution)/shard_map/ppermute | solution.py:356
